TPU v7x, 256 devices: a whole 4x4x8 slice. The times are simulated.
256 devices in a mesh: sub: 2 (over core), row: 16 (over x, y), col: 8 (over z).
Axes of the slice: x: 4, y: 4, z: 8, core: 2. Of those that a mesh axis runs over, the one named last changes fastest.
Arguments:
- front: float32 [16384, 16384], P(('sub', 'row'), 'col'), as said below
- child_blocks: float32 [2, 8192, 8192], P('sub', 'row', 'col'), may hold values from -1 to 1
- child_map: int32 [2, 8192], replicated, may hold values from 0 to 16383, as said below
Outputs:
- factored: float32 [16384, 16384], P(('sub', 'row'), 'col')
Inputs may be any that keep to these rules, and one draw needn't show every extreme that they name: Each row of child_map is strictly increasing. Call block b the parent indices b * 32 to b * 32 + 31. Of the entries at positions k * 1024 to (k + 1) * 1024 - 1 of a row, exactly 128 lie in blocks whose number modulo 8 is d, for every k and d. Of the entries at positions k * 512 to (k + 1) * 512 - 1, at most 24 lie in blocks whose number modulo 32 is p, for every k and p; for each child some p takes exactly 24 from every k. The front's diagonal dominates the rows of the pivot block by construction.
All inputs are finite; a program needn't handle non-finite values.
Results may differ from a plain program's by a relative error of at most 0.00012.
Values sent between devices are 32-bit elements; how exact they have to be, the bound alone decides.
A program may use at most 128 MiB of HBM per device.

v0:
```python
import jax
import jax.numpy as jnp
from jax import lax
from jax.sharding import PartitionSpec as P

PW = 512
NB = 32


def from_root(value, axis, source):
    kept = jnp.where(lax.axis_index(axis) == source, value, 0).astype(value.dtype)
    return lax.psum(kept, axis)


def natural_index(local, group, groups):
    return (local // NB * groups + group) * NB + local % NB


def local_index(natural, groups):
    return natural // NB // groups * NB + natural % NB


def slot_ranks(owner, groups):
    member = (owner[:, None] == jnp.arange(groups, dtype=jnp.int32)[None, :]).astype(jnp.int32)
    return jnp.sum(jnp.cumsum(member, axis=0) * member, axis=1) - 1


def body(front, child_blocks, child_map):
    n_sub = lax.axis_size("sub")
    n_row = lax.axis_size("row")
    n_col = lax.axis_size("col")
    row_groups = n_sub * n_row
    row_group = lax.axis_index("sub") * n_row + lax.axis_index("row")
    col_group = lax.axis_index("col")
    local_rows, local_cols = front.shape
    natural_rows = natural_index(jnp.arange(local_rows, dtype=jnp.int32), row_group, row_groups)
    natural_cols = natural_index(jnp.arange(local_cols, dtype=jnp.int32), col_group, n_col)
    lower = natural_rows[:, None] >= natural_cols[None, :]
    assembled = jnp.where(lower, front, jnp.float32(0.0))
    contribution = child_blocks[0]
    child_rows, child_cols = contribution.shape
    own_map = lax.dynamic_index_in_dim(child_map, lax.axis_index("sub"), 0, keepdims=False)
    row_start = lax.axis_index("row") * child_rows
    col_start = col_group * child_cols
    child_row_ids = row_start + jnp.arange(child_rows, dtype=jnp.int32)
    child_col_ids = col_start + jnp.arange(child_cols, dtype=jnp.int32)
    contribution = jnp.where(
        child_row_ids[:, None] >= child_col_ids[None, :], contribution, jnp.float32(0.0)
    )
    row_targets = lax.dynamic_slice_in_dim(own_map, row_start, child_rows)
    col_targets = lax.dynamic_slice_in_dim(own_map, col_start, child_cols)
    per_dest = child_cols // n_col
    col_owner = col_targets // NB % n_col
    col_slots = col_owner * per_dest + slot_ranks(col_owner, n_col)
    col_order = (
        jnp.zeros((child_cols,), jnp.int32)
        .at[col_slots]
        .set(jnp.arange(child_cols, dtype=jnp.int32))
    )
    spans = 2 * child_rows // NB // row_groups
    capacity = NB // 2 * spans + NB // 4 * max(0, 2 - spans)
    buffer_rows = row_groups * capacity
    row_owner = row_targets // NB % row_groups
    row_slots = row_owner * capacity + slot_ranks(row_owner, row_groups)
    source_rows = (
        jnp.full((buffer_rows,), child_rows, jnp.int32)
        .at[row_slots]
        .set(jnp.arange(child_rows, dtype=jnp.int32))
    )
    filled = source_rows < child_rows
    source_rows = jnp.minimum(source_rows, child_rows - 1)
    by_column = contribution[:, col_order]
    moved = lax.all_to_all(by_column, "col", split_axis=1, concat_axis=1, tiled=True)
    packed = jnp.where(filled[:, None], moved[source_rows], jnp.float32(0.0))
    received = lax.all_to_all(packed, ("sub", "row"), split_axis=0, concat_axis=0, tiled=True)
    slots_child = n_row * capacity
    received_cols = received.shape[1]
    received = received.reshape(n_sub, slots_child, received_cols)
    for child in range(n_sub):
        full_map = child_map[child]
        col_mask = full_map // NB % n_col == col_group
        taken = jnp.nonzero(col_mask, size=received_cols)[0]
        col_index = local_index(full_map[taken], n_col)
        match = (
            (full_map // NB % row_groups == row_group).astype(jnp.int32).reshape(n_row, child_rows)
        )
        ranks = jnp.cumsum(match, axis=1) - 1
        slots = jnp.arange(n_row, dtype=jnp.int32)[:, None] * capacity + ranks
        slots = jnp.where(match > 0, slots, slots_child).reshape(-1)
        row_index = (
            jnp.full((slots_child,), local_rows, jnp.int32)
            .at[slots]
            .set(local_index(full_map, row_groups), mode="drop")
        )
        slot_of_row = (
            jnp.full((local_rows,), slots_child, jnp.int32)
            .at[row_index]
            .set(jnp.arange(slots_child, dtype=jnp.int32), mode="drop")
        )
        col_source = (
            jnp.full((local_cols,), received_cols, jnp.int32)
            .at[col_index]
            .set(jnp.arange(received_cols, dtype=jnp.int32), mode="drop")
        )
        row_inside = slot_of_row < slots_child
        col_inside = col_source < received_cols
        placed = received[child][jnp.minimum(slot_of_row, slots_child - 1)][
            :, jnp.minimum(col_source, received_cols - 1)
        ]
        assembled = assembled + jnp.where(
            row_inside[:, None] & col_inside[None, :], placed, jnp.float32(0.0)
        )
    panel_local = PW // n_col
    gathered = lax.all_gather(assembled[:, :panel_local], "col", axis=1, tiled=True)
    panel = (
        gathered.reshape(local_rows, n_col, panel_local // NB, NB)
        .transpose(0, 2, 1, 3)
        .reshape(local_rows, PW)
    )
    head_blocks = max(1, PW // (row_groups * NB))
    heading = lax.all_gather(panel[: head_blocks * NB], ("sub", "row"), axis=0, tiled=True)
    corner = (
        heading.reshape(row_groups, head_blocks, NB, PW).transpose(1, 0, 2, 3).reshape(-1, PW)[:PW]
    )
    pivot = jnp.tril(corner) + jnp.tril(corner, -1).T
    factor = jnp.linalg.cholesky(pivot)
    solved = lax.linalg.triangular_solve(
        factor, panel, left_side=False, lower=True, transpose_a=True
    )
    factor_rows = jnp.where(
        natural_rows[:, None] < PW, factor[jnp.clip(natural_rows, 0, PW - 1)], solved
    )
    spread = row_groups // n_col
    pieces = [
        from_root(factor_rows, ("sub", "row"), col_group + step * n_col) for step in range(spread)
    ]
    stacked = jnp.stack([piece.reshape(local_rows // NB, NB, PW) for piece in pieces], axis=1)
    factor_cols = stacked.reshape(local_cols, PW)
    product = lax.dot_general(
        factor_rows,
        factor_cols,
        (((1,), (1,)), ((), ())),
        precision=lax.Precision.HIGHEST,
        preferred_element_type=jnp.float32,
    )
    update = assembled - product
    update = update.at[:, :panel_local].set(factor_rows[:, natural_cols[:panel_local]])
    return jnp.where(lower, update, jnp.float32(0.0))


def solution(mesh):
    return jax.shard_map(
        body,
        mesh=mesh,
        in_specs=(P(("sub", "row"), "col"), P("sub", "row", "col"), P()),
        out_specs=P(("sub", "row"), "col"),
        check_vma=False,
    )
```

profile of v0, /device:TPU:132, one launch (start us, length us, event | category | flops | bytes accessed | tf_op | source)
XLA Modules:
  0.0 715.7 jit_solution(14528451676120354646)
XLA Ops:
  11.0 4.3 scatter_custom_fusion.5
  20.1 4.9 gather_fusion.1
  25.0 7.3 %all-to-all-start = ((f32[512,8,128]{0,2,1:T(8,128)}), f32[512,8,128]{0,2,1:T(8,128)S(1)}, u32[]{:S(2)}, u32[]{:S(2)}) async-start(f32[512,8,128]{0,2,1:T(8,128)} %bitcast.218), calls=%async_computation | async-start | bytes 4194304 | tf_op jit(solution)/shard_map/all_to_all | solution.py:73
  38.1 56.9 %scatter_custom_fusion.2 = s32[1024]{0:T(1024)S(1)} fusion(s32[8192]{0:T(1024)S(1)} %bitcast.238, s32[8192]{0:T(1024)S(1)} %ne.666, s32[]{:T(128)} %constant.510.clone.1), kind=kCustom, calls=%fused_computation.418 | custom fusion | flops 8192 | bytes 4100 | tf_op jit(solution)/shard_map/scatter-add | solution.py:82
  100.4 6.2 gather_fusion
  106.5 56.9 %scatter_custom_fusion.8 = s32[1024]{0:T(1024)S(1)} fusion(s32[8192]{0:T(1024)S(1)} %bitcast.237, s32[8192]{0:T(1024)S(1)} %ne.666, s32[]{:T(128)} %constant.510.clone.1), kind=kCustom, calls=%fused_computation.416 | custom fusion | flops 8192 | bytes 4100 | tf_op jit(solution)/shard_map/scatter-add | solution.py:82
  164.8 6.2 gather_fusion.5
  171.5 30.6 %scatter_custom_fusion = s32[384]{0:T(512)S(1)} fusion(s32[8192]{0:T(1024)S(1)} %bitcast.236, s32[8192]{0:T(1024)S(1)} %get-tuple-element.71, s32[]{:T(128)} %constant.522.clone.1), kind=kCustom, calls=%fused_computation.433 | custom fusion | bytes 1540 | tf_op jit(solution)/shard_map/scatter | solution.py:93
  209.1 3.8 broadcast_select_fusion
  212.9 7.6 %all-to-all-start.1 = ((f32[32,24,1024]{2,1,0:T(8,128)}), f32[32,24,1024]{2,1,0:T(8,128)}, u32[]{:S(2)}, u32[]{:S(2)}) async-start(f32[32,24,1024]{2,1,0:T(8,128)} %broadcast_select_fusion), calls=%async_computation.1 | async-start | bytes 6291456 | tf_op jit(solution)/shard_map/all_to_all | solution.py:75
  220.7 4.3 scatter_custom_fusion.3
  225.0 30.4 %scatter_custom_fusion.6 = s32[384]{0:T(512)S(1)} fusion(s32[8192]{0:T(1024)S(1)} %bitcast.235, s32[8192]{0:T(1024)S(1)} %get-tuple-element.68, s32[]{:T(128)} %constant.522.clone.1), kind=kCustom, calls=%fused_computation.431 | custom fusion | bytes 1540 | tf_op jit(solution)/shard_map/scatter | solution.py:93
  261.4 4.3 scatter_custom_fusion.9
  273.9 8.9 %gather_fusion.4 = f32[2048,512]{1,0:T(8,128)} fusion(f32[512,1024]{0,1:T(8,128)S(1)} %copy.59, s32[2048]{0:T(1024)S(1)} %fusion.85), kind=kCustom, calls=%fused_computation.4 | custom fusion | bytes 8396800 | tf_op jit(solution)/shard_map/gather | solution.py:107
  282.8 5.5 copy.60
  292.8 8.9 %gather_fusion.7 = f32[2048,512]{1,0:T(8,128)} fusion(f32[512,1024]{0,1:T(8,128)S(1)} %copy.66, s32[2048]{0:T(1024)S(1)} %fusion.86), kind=kCustom, calls=%fused_computation.7 | custom fusion | bytes 8396800 | tf_op jit(solution)/shard_map/gather | solution.py:107
  301.7 5.4 copy.67
  307.1 5.6 fusion.1
  315.6 37.3 %all-gather.3.cloned.1.call-done = f32[512,512]{0,1:T(8,128)} async-done(((f32[512,64]{0,1:T(8,128)}), f32[512,512]{0,1:T(8,128)}) %all-gather.3.cloned.1.call-update) | async-done | bytes 1048592 | tf_op jit(solution)/shard_map/all_gather | solution.py:114
  358.6 46.4 %all-gather.5.cloned.1.call-done = f32[1024,512]{1,0:T(8,128)} async-done(((f32[32,512]{1,0:T(8,128)}), f32[1024,512]{1,0:T(8,128)}) %all-gather.5.cloned.1.call-update) | async-done | bytes 2097168 | tf_op jit(solution)/shard_map/all_gather | solution.py:121
  409.7 11.7 %cholesky.103 = f32[128,128]{1,0:T(8,128)S(1)} custom-call(f32[128,128]{1,0:T(8,128)S(1)} %cholesky.263), custom_call_target="Cholesky" | custom-call | tf_op jit(solution)/shard_map/jit(cholesky)/cholesky | solution.py:126
  421.6 9.8 %custom-call.30 = f32[1,128,128]{1,2,0:T(8,128)S(1)} custom-call(f32[1,128,128]{2,1,0:T(8,128)S(1)} %get-tuple-element.62), custom_call_target="InvertDiagBlocksLowerTriangular" | custom-call | tf_op jit(solution)/shard_map/jit(cholesky)/cholesky | solution.py:126
  433.9 11.7 %cholesky.215 = f32[128,128]{1,0:T(8,128)S(1)} custom-call(f32[128,128]{1,0:T(8,128)S(1)} %cholesky.267), custom_call_target="Cholesky" | custom-call | tf_op jit(solution)/shard_map/jit(cholesky)/cholesky | solution.py:126
  447.0 10.0 %custom-call.31 = f32[1,128,128]{1,2,0:T(8,128)S(1)} custom-call(f32[1,128,128]{2,1,0:T(8,128)S(1)} %get-tuple-element.59), custom_call_target="InvertDiagBlocksLowerTriangular" | custom-call | tf_op jit(solution)/shard_map/jit(cholesky)/cholesky | solution.py:126
  458.5 11.7 %cholesky.236 = f32[128,128]{1,0:T(8,128)S(1)} custom-call(f32[128,128]{1,0:T(8,128)S(1)} %cholesky.272), custom_call_target="Cholesky" | custom-call | tf_op jit(solution)/shard_map/jit(cholesky)/cholesky | solution.py:126
  471.0 9.8 %custom-call.32 = f32[1,128,128]{1,2,0:T(8,128)S(1)} custom-call(f32[1,128,128]{2,1,0:T(8,128)S(1)} %get-tuple-element.56), custom_call_target="InvertDiagBlocksLowerTriangular" | custom-call | tf_op jit(solution)/shard_map/jit(cholesky)/cholesky | solution.py:126
  482.3 11.9 %cholesky.253 = f32[128,128]{1,0:T(8,128)S(1)} custom-call(f32[128,128]{1,0:T(8,128)S(1)} %convolution_subtract_fusion.6), custom_call_target="Cholesky" | custom-call | tf_op jit(solution)/shard_map/jit(cholesky)/cholesky | solution.py:126
  498.8 14.1 %while.2 = (s32[]{:T(128)}, f32[512,512]{1,0:T(8,128)}, s32[4,2]{0,1:T(2,128)S(1)}, f32[4,128,128]{2,1,0:T(8,128)}, s32[]{:T(128)}) while((s32[]{:T(128)}, f32[512,512]{1,0:T(8,128)}, s32[4,2]{0,1:T(2,128)S(1)}, f32[4,128,128]{2,1,0:T(8,128)}, s32[]{:T(128)}) %tuple.45), condition=%wide.while_cond.1, body=%wide.while_body.1.sunk | while | flops 2 | bytes 132705 | solution.py:127
  512.8 40.1 %custom-call.33 = f32[4,128,128]{1,2,0:T(8,128)S(1)} custom-call(f32[4,128,128]{2,1,0:T(8,128)} %get-tuple-element.24), custom_call_target="InvertDiagBlocksLowerTriangular" | custom-call | tf_op jit(solution)/shard_map/triangular_solve | solution.py:127
  570.1 119.3 %all-reduce.4.cloned.1.call-done = (f32[16,1,32,512]{3,2,1,0:T(8,128)}, f32[16,1,32,512]{3,2,1,0:T(8,128)}, f32[16,1,32,512]{3,2,1,0:T(8,128)}, f32[16,1,32,512]{3,2,1,0:T(8,128)}) async-done(((f32[16,1,32,512]{3,2,1,0:T(8,128)}, f32[16,1,32,512]{3,2,1,0:T(8,128)}, f32[16,1,32,512]{3,2,1,0:T(8,128)}, f32[16,1,32,512]{3,2,1,0:T(8,128)}), (f32[16,1,32,512]{3,2,1,0:T(8,128)}, f32[16,1,32,512]{3,2,1,0:T(8,128)}, ...) | async-done | bytes 4194320 | tf_op jit(solution)/shard_map/psum | solution.py:12
  692.9 6.8 convolution_subtract_fusion
  704.2 4.6 compare_select_fusion
  (211 shorter events, 109.3 us)
Async XLA Ops:
  25.0 7.3 %copy-start.7 = (s32[2,8192]{1,0:T(2,128)S(1)}, s32[2,8192]{1,0:T(2,128)}, u32[]{:S(2)}) copy-start(s32[2,8192]{1,0:T(2,128)} %param.7) | copy-start | bytes 196612
  25.0 177.3 %all-to-all-start = ((f32[512,8,128]{0,2,1:T(8,128)}), f32[512,8,128]{0,2,1:T(8,128)S(1)}, u32[]{:S(2)}, u32[]{:S(2)}) async-start(f32[512,8,128]{0,2,1:T(8,128)} %bitcast.218), calls=%async_computation | async-start | bytes 4194304 | tf_op jit(solution)/shard_map/all_to_all | solution.py:73
  202.2 1.3 copy-start.4
  212.9 53.0 %all-to-all-start.1 = ((f32[32,24,1024]{2,1,0:T(8,128)}), f32[32,24,1024]{2,1,0:T(8,128)}, u32[]{:S(2)}, u32[]{:S(2)}) async-start(f32[32,24,1024]{2,1,0:T(8,128)} %broadcast_select_fusion), calls=%async_computation.1 | async-start | bytes 6291456 | tf_op jit(solution)/shard_map/all_to_all | solution.py:75
  220.6 132.3 %all-gather.3.cloned.1.call-start = ((), (), s32[]{:S(2)}) async-start(), calls=%async_computation.2 | async-start | bytes 1179648 | tf_op jit(solution)/shard_map/all_gather | solution.py:114
  282.8 5.5 copy-start
  312.7 2.0 copy-start.1
  315.6 89.5 %all-gather.5.cloned.1.call-start = ((), (), s32[]{:S(2)}) async-start(), calls=%async_computation.3 | async-start | bytes 2162688 | tf_op jit(solution)/shard_map/all_gather | solution.py:121
  354.8 334.6 %all-reduce.4.cloned.1.call-start = ((), (), s32[]{:S(2)}) async-start(), calls=%async_computation.4 | async-start | bytes 8388608 | tf_op jit(solution)/shard_map/psum | solution.py:12
  408.7 1.0 copy-start.5
  498.7 61.2 %copy-start.6 = (f32[512,128]{1,0:T(8,128)S(1)}, f32[512,128]{1,0:T(8,128)}, u32[]{:S(2)}) copy-start(f32[512,128]{1,0:T(8,128)} %copy.90) | copy-start | bytes 786436
  553.0 0.7 copy-start.8
  689.4 3.4 copy-start.2
  699.7 2.0 copy-start.3
Sparse Core Ops, SparseCore 0:
  315.7 37.1 all-gather.2
  355.4 49.5 all-gather.4
  568.3 121.1 all-reduce.3
where the time goes:
time: 728 us; the launch traced here: 716 us
  other arithmetic  273 us (38%)
  waiting for transfers between devices  203 us (28%)
  local copies, waits for them, and re-layouts  185 us (25%)
  matrix products  22.3 us (3%)
  between operations  17.1 us (2%)
  starting transfers between devices  15.6 us (2%)
    psum x1, waiting for transfers between devices, from_root(): return lax.psum(kept, axis)  119 us
    scatter-add x2, other arithmetic, body(): taken = jnp.nonzero(col_mask, size=received_cols)[0]  114 us
    another operation x15, other arithmetic, body(): factor = jnp.linalg.cholesky(pivot)  79.5 us
    scatter x2, local copies, waits for them, and re-layouts, body(): row_index = jnp.full((slots_child,), local_rows, jnp.int32).at[slots].set...  61.1 us
    all_gather x1, waiting for transfers between devices, body(): lax.all_gather(panel[:head_blocks * NB], ('sub', 'row'), axis=0, tiled=True)  46.4 us
    another operation x3, other arithmetic, body(): lax.linalg.triangular_solve(factor, panel, left_side=False, lower=True, t...  41.4 us
    gather x8, local copies, waits for them, and re-layouts, body(): received[child][jnp.minimum(slot_of_row, slots_child - 1)]  37.8 us
    all_gather x1, waiting for transfers between devices, body(): lax.all_gather(assembled[:, :panel_local], 'col', axis=1, tiled=True)  37.3 us
  transfers between devices with their start and end apart: 5, of which 3 were waited for; matrix products, arithmetic and copies ran while one was open for 31% of the time, Pallas kernels for 0%

commit v1 on v0

v1 whole, which is shorter than its diff:
```python
import functools

import jax
import jax.numpy as jnp
from jax import lax
from jax.experimental import pallas as pl
from jax.experimental.pallas import tpu as pltpu
from jax.sharding import PartitionSpec as P

PW = 512
NB = 32
CAP = 24
F32 = jnp.float32
BF16 = jnp.bfloat16
I32 = jnp.int32
AXES = ("sub", "row", "col")


def iota(shape, dim):
    return lax.broadcasted_iota(I32, shape, dim)


def onehot(cond):
    return jnp.where(cond, F32(1.0), F32(0.0)).astype(BF16)


def split(value):
    high = value.astype(BF16)
    return high, (value - high.astype(F32)).astype(BF16)


def mm(a, b):
    return lax.dot_general(a, b, (((1,), (0,)), ((), ())), preferred_element_type=F32)


def mt(a, b):
    return lax.dot_general(a, b, (((1,), (1,)), ((), ())), preferred_element_type=F32)


def params(mib=None):
    return pltpu.CompilerParams(vmem_limit_bytes=None if mib is None else mib << 20)


VM = pl.BlockSpec(memory_space=pltpu.VMEM)
SM = pl.BlockSpec(memory_space=pltpu.SMEM)


def ranks_of(owner, groups, rows):
    n = owner.shape[1]
    member = jnp.where(owner == iota((rows, n), 0), F32(1.0), F32(0.0))
    upto = onehot(iota((n, n), 0) <= iota((n, n), 1))
    counts = mm(member.astype(BF16), upto)
    return (jnp.sum(counts * member, axis=0, keepdims=True) - 1.0).astype(I32)


def columns_kernel(at_ref, map_ref, x_ref, o_ref):
    rows, cols = x_ref.shape
    row0, col0 = at_ref[0], at_ref[1]
    keep = row0 + iota((rows, cols), 0) >= col0 + iota((rows, cols), 1)
    high, low = split(jnp.where(keep, x_ref[...], F32(0.0)))
    owner = (map_ref[...] >> 5) & 7
    slot = owner * 128 + ranks_of(owner, 8, 16)
    for pair in range(4):
        pick = onehot(slot == pair * 256 + iota((256, cols), 0))
        out = mt(high, pick) + mt(low, pick)
        o_ref[2 * pair] = out[:, :128]
        o_ref[2 * pair + 1] = out[:, 128:]


def rows_kernel(map_ref, x_ref, o_ref, p_ref):
    owner = (map_ref[...] >> 5) & 31
    slot = owner * CAP + ranks_of(owner, 32, 32)
    n = owner.shape[1]
    pick = onehot(slot == iota((32 * CAP, n), 0))
    for pair in range(4):
        high, low = split(jnp.concatenate([x_ref[2 * pair], x_ref[2 * pair + 1]], axis=1))
        out = mm(pick, high) + mm(pick, low)
        o_ref[:, pl.ds(pair * 256, 256)] = out
        if pair == 0:
            p_ref[...] = out[:, :128]


def index_kernel(at_ref, map_ref, slot_ref, col_ref):
    rg, cg = at_ref[0], at_ref[1]
    upto = onehot(iota((512, 512), 0) <= iota((512, 512), 1))
    before64 = onehot(iota((64, 64), 1) < iota((64, 64), 0))
    before32 = onehot(iota((32, 32), 0) < iota((32, 32), 1))
    for child in range(2):
        full = map_ref[child]
        match = onehot(((full >> 5) & 31) == rg)
        counts = mm(match, upto)
        slots = jnp.zeros((NB, 16), F32)
        present = jnp.zeros((64, NB), F32)
        for k in range(16):
            here = full[k : k + 1, :]
            block = here >> 5
            off = jnp.where((here & 31) == iota((NB, 512), 0), F32(1.0), F32(0.0))
            own_rows = onehot(
                jnp.where((block & 31) == rg, block >> 5, -1) == iota((16, 512), 0)
            )
            ranked = (off * counts[k : k + 1, :]).astype(BF16)
            off = off.astype(BF16)
            slots = slots + mt(ranked, own_rows) + F32(k * CAP) * mt(off, own_rows)
            own_cols = onehot(jnp.where((block & 7) == cg, block >> 3, -1) == iota((64, 512), 0))
            present = present + mt(own_cols, off)
        slot_ref[child] = slots.astype(I32) - 1
        pb = present.astype(BF16)
        ahead = jnp.sum(mm(before64, pb), axis=1, keepdims=True)
        place = ahead + mm(pb, before32)
        col_ref[child] = jnp.where(present > 0.5, place.astype(I32), -1)


def natural_lower(rg, cg, rows, cols, col0):
    r, c = iota((rows, cols), 0), col0 + iota((rows, cols), 1)
    nat_row = ((r >> 5) * 32 + rg) * 32 + (r & 31)
    nat_col = ((c >> 5) * 8 + cg) * 32 + (c & 31)
    return nat_row >= nat_col


def row_picker(slots, n):
    parts = [onehot(slots[:, b : b + 1] == iota((NB, n), 1)) for b in range(16)]
    return jnp.concatenate(parts, axis=0)


def panel_kernel(at_ref, slot_ref, col_ref, x_ref, front_ref, o_ref):
    rg, cg = at_ref[0], at_ref[1]
    total = jnp.where(natural_lower(rg, cg, 512, 128, 0), front_ref[...], F32(0.0))
    n = x_ref.shape[1]
    for child in range(2):
        pick = row_picker(slot_ref[child], n)
        high, low = split(x_ref[child])
        high, low = split(mm(pick, high) + mm(pick, low))
        put = onehot(col_ref[child] == iota((128, 128), 0))
        total = total + mm(high, put) + mm(low, put)
    left = iota((64, 128), 1) < 64
    for t in range(4):
        a = total[t * 128 : t * 128 + 64]
        b = total[t * 128 + 64 : t * 128 + 128]
        o_ref[t * 64 : t * 64 + 64, :] = jnp.where(left, a, pltpu.roll(b, 64, 1))


def sweep(w):
    tiles = [w[8 * i : 8 * i + 8, :] for i in range(16)]
    lane = iota((8, 128), 1)
    sub = iota((8, 128), 0)
    for k in range(128):
        own, s = k // 8, k % 8
        row = tiles[own][s : s + 1, :]
        inv = 1.0 / row[:, k : k + 1]
        pivot_row = jnp.where(lane[:1] == k, F32(1.0), row)
        scaled = pivot_row * inv
        for i in range(own, 16):
            t = tiles[i]
            col = t[:, k : k + 1]
            new = jnp.where(lane == k, F32(0.0), t) - col * scaled
            tiles[i] = jnp.where(sub > s, new, t) if i == own else new
    w = jnp.concatenate(tiles, axis=0)
    r, c = iota((128, 128), 0), iota((128, 128), 1)
    diag = jnp.sum(jnp.where(r == c, w, F32(0.0)), axis=1, keepdims=True)
    scale = 1.0 / jnp.sqrt(diag)
    upper = jnp.where(c >= r, w, F32(0.0)) * scale
    inverse = jnp.where(c < r, w, jnp.where(c == r, F32(1.0), F32(0.0))) * scale
    return upper, inverse


def exact(a, b, dims):
    return lax.dot_general(
        a, b, (dims, ((), ())), precision=lax.Precision.HIGHEST, preferred_element_type=F32
    )


def factor_kernel(s_ref, low_ref, inv_ref, w_ref):
    r, c = iota((PW, PW), 0), iota((PW, PW), 1)
    raw = s_ref[...]
    w_ref[:, :PW] = jnp.where(r >= c, raw, F32(0.0)) + jnp.where(r > c, raw, F32(0.0)).T
    w_ref[:, PW:] = jnp.where(r == c, F32(1.0), F32(0.0))

    def step(kb, carry):
        at = pl.multiple_of(kb * 128, 128)
        upper, inverse = sweep(w_ref[pl.ds(at, 128), pl.ds(at, 128)])
        rows = exact(inverse, w_ref[pl.ds(at, 128), :], ((1,), (0,)))
        lanes = iota((128, PW), 1)
        ahead = jnp.where(lanes >= at + 128, rows[:, :PW], F32(0.0))
        w_ref[...] = w_ref[...] - exact(ahead, rows, ((0,), (0,)))
        w_ref[pl.ds(at, 128), :] = jnp.concatenate([ahead, rows[:, PW:]], axis=1)
        w_ref[pl.ds(at, 128), pl.ds(at, 128)] = upper
        return carry

    lax.fori_loop(0, PW // 128, step, 0)
    low_ref[...] = w_ref[:, :PW].T
    turned = w_ref[:, PW:].T
    for c8 in range(8):
        for half in range(2):
            src = (half * 8 + c8) * NB
            inv_ref[(c8 * 2 + half) * NB : (c8 * 2 + half + 1) * NB, :] = turned[src : src + NB, :]


def unpack(pieces, left):
    top, bottom = [], []
    for p in range(4):
        a, b = pieces[2 * p], pieces[2 * p + 1]
        top.append(jnp.where(left, a, pltpu.roll(b, 64, 1)))
        bottom.append(jnp.where(left, pltpu.roll(a, 64, 1), b))
    return jnp.concatenate(
        [jnp.concatenate(top, axis=1), jnp.concatenate(bottom, axis=1)], axis=0
    )


def three(a, b, dot):
    return dot(a[0], b[0]) + (dot(a[0], b[1]) + dot(a[1], b[0]))


def final_kernel(
    at_ref, slot_ref, col_ref, x_ref, front_ref, own_ref, cols_ref, inv_ref, low_ref,
    o_ref, ih, il, fh, fl, yh, yl, panel_ref,
):
    rg, cg = at_ref[0], at_ref[1]
    ct = pl.program_id(0)
    left = iota((64, 128), 1) < 64

    @pl.when(ct == 0)
    def _():
        ih[...], il[...] = split(inv_ref[...])
        inv = ih[...], il[...]
        for t in range(4):
            tile = unpack([own_ref[c, t * 64 : t * 64 + 64, :] for c in range(8)], left)
            rows = three(split(tile), inv, mm)
            if t == 0:
                keep = (iota((128, PW), 0) < NB) & (rg < 16)
                known = jnp.concatenate([low_ref[...], jnp.zeros((128 - NB, PW), F32)], axis=0)
                rows = jnp.where(keep, known, rows)
            fh[t * 128 : t * 128 + 128, :], fl[t * 128 : t * 128 + 128, :] = split(rows)
        lane = iota((PW, 128), 1)
        nat = ((lane >> 5) * 8 + cg) * 32 + (lane & 31)
        pick = onehot((nat == iota((PW, 128), 0)) & (lane < 64))
        panel_ref[...] = mm(fh[...], pick) + mm(fl[...], pick)
        n = x_ref.shape[1]
        for child in range(2):
            pick = row_picker(slot_ref[child], n)
            high, low = split(x_ref[child])
            yh[child], yl[child] = split(mm(pick, high) + mm(pick, low))

    inv = ih[...], il[...]
    parts = []
    for i in range(4):
        tile = unpack([cols_ref[i * 8 + c] for c in range(8)], left)
        parts.append(three(split(tile), inv, mm))
    cols = jnp.concatenate(
        [parts[i][q * NB : q * NB + NB] for q in range(4) for i in range(4)], axis=0
    )
    total = front_ref[...] - three((fh[...], fl[...]), split(cols), mt)
    for child in range(2):
        put = onehot(col_ref[child] == iota((1024, 512), 0))
        total = total + mm(yh[child], put) + mm(yl[child], put)
    total = jnp.where(natural_lower(rg, cg, 512, 512, ct * 512), total, F32(0.0))
    o_ref[...] = total

    @pl.when(ct == 0)
    def _():
        lane = iota((512, 128), 1)
        value = jnp.where(
            natural_lower(rg, cg, 512, 128, 0), panel_ref[...], F32(0.0)
        )
        o_ref[:, :128] = jnp.where(lane < 64, value, total[:, :128])


def body(front, child_blocks, child_map):
    sub, row, cg = lax.axis_index("sub"), lax.axis_index("row"), lax.axis_index("col")
    rg = sub * 16 + row
    at = jnp.stack([rg, cg]).astype(I32)
    own_map = lax.dynamic_index_in_dim(child_map, sub, 0, keepdims=True)
    row_targets = lax.dynamic_slice_in_dim(own_map, row * 512, 512, axis=1)
    col_targets = lax.dynamic_slice_in_dim(own_map, cg * 1024, 1024, axis=1)
    start = jnp.stack([row * 512, cg * 1024]).astype(I32)

    by_column = pl.pallas_call(
        columns_kernel,
        out_shape=jax.ShapeDtypeStruct((8, 512, 128), F32),
        in_specs=[SM, VM, VM],
        out_specs=VM,
        name="columns",
        compiler_params=params(40),
    )(start, col_targets, child_blocks[0])
    moved = lax.all_to_all(by_column, "col", split_axis=0, concat_axis=0, tiled=True)

    slots, cols = pl.pallas_call(
        index_kernel,
        out_shape=(
            jax.ShapeDtypeStruct((2, NB, 16), I32),
            jax.ShapeDtypeStruct((2, 64, NB), I32),
        ),
        in_specs=[SM, VM],
        out_specs=(VM, VM),
        name="index",
        compiler_params=params(40),
        cost_estimate=pl.CostEstimate(flops=10**8, bytes_accessed=10**7, transcendentals=0),
    )(at, child_map.reshape(2, 16, 512))
    cols = cols.reshape(2, 1, 2048)

    packed, packed_panel = pl.pallas_call(
        rows_kernel,
        out_shape=(
            jax.ShapeDtypeStruct((32 * CAP, 1024), F32),
            jax.ShapeDtypeStruct((32 * CAP, 128), F32),
        ),
        in_specs=[VM, VM],
        out_specs=(VM, VM),
        name="rows",
        compiler_params=params(40),
    )(row_targets, moved)
    got_panel = lax.all_to_all(
        packed_panel.reshape(32, CAP, 128), ("sub", "row"), split_axis=0, concat_axis=0, tiled=True
    )
    packed, got_panel = lax.optimization_barrier((packed, got_panel))
    received = lax.all_to_all(
        packed.reshape(32, CAP, 1024), ("sub", "row"), split_axis=0, concat_axis=0, tiled=True
    )

    piece = pl.pallas_call(
        panel_kernel,
        out_shape=jax.ShapeDtypeStruct((256, 128), F32),
        grid=(1,),
        in_specs=[
            SM,
            pl.BlockSpec((2, NB, 16), lambda i: (0, 0, 0)),
            pl.BlockSpec((2, 1, 128), lambda i: (0, 0, 0)),
            pl.BlockSpec((2, 16 * CAP, 128), lambda i: (0, 0, 0)),
            pl.BlockSpec((512, 128), lambda i: (0, 0)),
        ],
        out_specs=pl.BlockSpec((256, 128), lambda i: (0, 0)),
        name="panel",
        compiler_params=params(40),
    )(at, slots, cols, got_panel.reshape(2, 16 * CAP, 128), front)

    head = lax.all_gather(piece[:NB, :64], AXES, axis=0)
    head = head.reshape(32, 8, NB, 2, NB)[:16].transpose(0, 2, 3, 1, 4).reshape(PW, PW)
    own_rows = lax.all_gather(piece, "col", axis=0)
    swaps = [
        ((8 * i + a) * 8 + b, (8 * i + b) * 8 + a)
        for i in range(4)
        for a in range(8)
        for b in range(8)
    ]
    swapped = lax.ppermute(piece, AXES, swaps)
    col_rows = lax.all_gather(swapped, ("sub", "row"), axis=0)

    lower, inverse = pl.pallas_call(
        factor_kernel,
        out_shape=(
            jax.ShapeDtypeStruct((PW, PW), F32),
            jax.ShapeDtypeStruct((PW, PW), F32),
        ),
        in_specs=[VM],
        out_specs=(VM, VM),
        scratch_shapes=[pltpu.VMEM((PW, 2 * PW), F32)],
        name="factor",
        compiler_params=params(40),
        cost_estimate=pl.CostEstimate(flops=3 * 10**10, bytes_accessed=10**8, transcendentals=0),
    )(head)

    return pl.pallas_call(
        final_kernel,
        out_shape=jax.ShapeDtypeStruct((512, 2048), F32),
        grid=(4,),
        in_specs=[
            SM,
            pl.BlockSpec((2, NB, 16), lambda i: (0, 0, 0)),
            pl.BlockSpec((2, 1, 512), lambda i: (0, 0, i)),
            pl.BlockSpec((2, 16 * CAP, 1024), lambda i: (0, 0, 0)),
            pl.BlockSpec((512, 512), lambda i: (0, i)),
            pl.BlockSpec((8, 256, 128), lambda i: (0, 0, 0)),
            pl.BlockSpec((32, 64, 128), lambda i: (0, i, 0)),
            pl.BlockSpec((PW, PW), lambda i: (0, 0)),
            pl.BlockSpec((NB, PW), lambda i: (0, 0)),
        ],
        out_specs=pl.BlockSpec((512, 512), lambda i: (0, i)),
        scratch_shapes=[
            pltpu.VMEM((PW, PW), BF16),
            pltpu.VMEM((PW, PW), BF16),
            pltpu.VMEM((512, PW), BF16),
            pltpu.VMEM((512, PW), BF16),
            pltpu.VMEM((2, 512, 1024), BF16),
            pltpu.VMEM((2, 512, 1024), BF16),
            pltpu.VMEM((512, 128), F32),
        ],
        name="final",
        compiler_params=params(60),
    )(
        at,
        slots,
        cols,
        received.reshape(2, 16 * CAP, 1024),
        front,
        own_rows,
        col_rows,
        inverse,
        lax.dynamic_slice_in_dim(lower, jnp.minimum(rg, 15) * NB, NB, axis=0),
    )


def solution(mesh):
    return jax.shard_map(
        body,
        mesh=mesh,
        in_specs=(P(("sub", "row"), "col"), P("sub", "row", "col"), P()),
        out_specs=P(("sub", "row"), "col"),
        check_vma=False,
    )
```

time: 728 us -> 344 us (0.47); the launches traced: 716 us -> 340 us
  other arithmetic: 273 us -> 0.15 us
  local copies, waits for them, and re-layouts: 185 us -> 22.9 us
  Pallas kernels: 0 us -> 91.2 us
  waiting for transfers between devices: 203 us -> 177 us
  matrix products: 22.3 us -> 0 us
  starting transfers between devices: 15.6 us -> 35.5 us
    another operation x41 -> x2, other arithmetic: 133 us -> 0.15 us  [the longest x1 0.08 us: body(): at = jnp.stack([rg, cg]).astype(I32)]
    psum x1 -> x0, waiting for transfers between devices: 119 us -> none  [from_root(): return lax.psum(kept, axis)]
    scatter-add x2 -> x0, other arithmetic: 114 us -> none  [body(): taken = jnp.nonzero(col_mask, size=received_cols)[0]]
    pallas_call x0 -> x6, Pallas kernels: none -> 91.2 us  [the longest x1 53.3 us: body(): pl.pallas_call(factor_kernel, out_shape=(jax.ShapeDtypeStruct((PW, PW), F...]
    scatter x9 -> x0, local copies, waits for them, and re-layouts: 84.1 us -> none  [the longest x2 61.1 us: body(): row_index = jnp.full((slots_child,), local_rows, jnp.int32).at[slots].set...]
    gather x15 -> x0, local copies, waits for them, and re-layouts: 61 us -> none  [the longest x8 37.8 us: body(): received[child][jnp.minimum(slot_of_row, slots_child - 1)]]
    all_to_all x2 -> x3, waiting for transfers between devices: 0.01 us -> 51.9 us  [the longest x1 45.8 us: body(): lax.all_to_all(by_column, 'col', split_axis=0, concat_axis=0, tiled=True)]
    all_gather x2 -> x3, waiting for transfers between devices: 83.7 us -> 120 us  [the longest x1 96.4 us: body(): head = lax.all_gather(piece[:NB, :64], AXES, axis=0)]
  transfers between devices with their start and end apart: 5 -> 7, of which waited for: 3 -> 5; matrix products, arithmetic and copies ran while one was open for 31% -> 4% of each run, Pallas kernels for 0% -> 16%
where the time goes in v1:
time: 344 us; the launch traced here: 340 us
  waiting for transfers between devices  177 us (51%)
  Pallas kernels  91.2 us (27%)
  starting transfers between devices  35.5 us (10%)
  local copies, waits for them, and re-layouts  22.9 us (7%)
  between operations  13.3 us (4%)
    all_gather x1, waiting for transfers between devices, body(): head = lax.all_gather(piece[:NB, :64], AXES, axis=0)  96.4 us
    pallas_call x1, Pallas kernels, body(): pl.pallas_call(factor_kernel, out_shape=(jax.ShapeDtypeStruct((PW, PW), F...  53.3 us
    all_to_all x1, waiting for transfers between devices, body(): lax.all_to_all(by_column, 'col', split_axis=0, concat_axis=0, tiled=True)  45.8 us
    pallas_call x1, Pallas kernels, body(): pl.pallas_call(final_kernel, out_shape=jax.ShapeDtypeStruct((512, 2048),...  24.9 us
    all_gather x1, waiting for transfers between devices, body(): col_rows = lax.all_gather(swapped, ('sub', 'row'), axis=0)  23.5 us
    all_to_all x1, starting transfers between devices, body(): lax.all_to_all(packed.reshape(32, CAP, 1024), ('sub', 'row'), split_axis=...  13 us
    ppermute x1, starting transfers between devices, body(): swapped = lax.ppermute(piece, AXES, swaps)  7.63 us
    all_to_all x1, starting transfers between devices, body(): lax.all_to_all(packed_panel.reshape(32, CAP, 128), ('sub', 'row'), split_...  7.6 us
  transfers between devices with their start and end apart: 7, of which 5 were waited for; matrix products, arithmetic and copies ran while one was open for 4% of the time, Pallas kernels for 16%

profile of v1, /device:TPU:132, one launch (start us, length us, event | category | flops | bytes accessed | tf_op | source)
XLA Modules:
  0.0 340.0 jit_solution(13722089413074396226)
XLA Ops:
  6.5 0.1 pad_add_fusion.1.at_ref
  6.6 0.8 dynamic_slice.12.map_ref
  7.4 1.6 copy-done.1
  9.0 4.7 %columns.1 = f32[8,512,128]{2,1,0:T(8,128)} custom-call(s32[2]{0:T(128)S(1)} %pad_add_fusion.1.at_ref, s32[1,1024]{1,0:T(1,128)S(1)} %dynamic_slice.12.map_ref, f32[512,1024]{1,0:T(8,128)S(1)} %bitcast.20), custom_call_target="tpu_custom_call" | custom-call | tf_op jit(solution)/shard_map/columns/pallas_call | solution.py:276
  13.7 7.2 %all-to-all-start = ((f32[8,512,128]{2,1,0:T(8,128)}), f32[8,512,128]{2,1,0:T(8,128)S(1)}, u32[]{:S(2)}, u32[]{:S(2)}) async-start(f32[8,512,128]{2,1,0:T(8,128)} %columns.1), calls=%async_computation | async-start | bytes 4194304 | tf_op jit(solution)/shard_map/all_to_all | solution.py:284
  20.9 0.1 dynamic_slice.11.map_ref
  21.0 45.8 %all-to-all-done.x_ref = f32[8,512,128]{2,1,0:T(8,128)S(1)} async-done(((f32[8,512,128]{2,1,0:T(8,128)}), f32[8,512,128]{2,1,0:T(8,128)S(1)}, u32[]{:S(2)}, u32[]{:S(2)}) %all-to-all-start) | async-done | bytes 2097184 | tf_op jit(solution)/shard_map/all_to_all | solution.py:284
  66.7 3.7 %rows.1 = (f32[768,1024]{1,0:T(8,128)}, f32[768,128]{1,0:T(8,128)}) custom-call(s32[1,512]{1,0:T(1,128)S(1)} %dynamic_slice.11.map_ref, f32[8,512,128]{2,1,0:T(8,128)S(1)} %all-to-all-done.x_ref), custom_call_target="tpu_custom_call" | custom-call | tf_op jit(solution)/shard_map/rows/pallas_call | solution.py:300
  70.4 7.6 %all-to-all-start.1 = ((f32[32,24,128]{2,1,0:T(8,128)}), f32[32,24,128]{2,1,0:T(8,128)S(1)}, u32[]{:S(2)}, u32[]{:S(2)}) async-start(f32[32,24,128]{2,1,0:T(8,128)} %bitcast.5), calls=%async_computation.1 | async-start | bytes 786432 | tf_op jit(solution)/shard_map/all_to_all | solution.py:311
  78.1 0.1 pad_add_fusion.at_ref
  78.2 2.4 index.1
  80.6 0.1 reshape.35.col_ref
  80.7 6.1 %all-to-all-done.1 = f32[32,24,128]{2,1,0:T(8,128)S(1)} async-done(((f32[32,24,128]{2,1,0:T(8,128)}), f32[32,24,128]{2,1,0:T(8,128)S(1)}, u32[]{:S(2)}, u32[]{:S(2)}) %all-to-all-start.1) | async-done | bytes 393248 | tf_op jit(solution)/shard_map/all_to_all | solution.py:311
  86.8 2.2 copy-done
  89.0 2.2 panel.1
  91.3 1.3 slice.13
  92.7 0.7 all-gather.7.cloned.1.call-update
  93.4 7.6 %collective-permute-start = (f32[256,128]{1,0:T(8,128)}, f32[256,128]{1,0:T(8,128)S(1)}, u32[]{:S(2)}, u32[]{:S(2)}) collective-permute-start(f32[256,128]{1,0:T(8,128)} %panel.1), channel_id=1, source_target_pairs={{0,0},{1,8},{2,16},{3,24},{4,32},{5,40},{6,48},{7,56},{8,1},{9,9},... | collective-permute-start | bytes 393224 | tf_op jit(solution)/shard_map/ppermute | solution.py:344
  101.0 4.4 %collective-permute-done = f32[256,128]{1,0:T(8,128)S(1)} collective-permute-done((f32[256,128]{1,0:T(8,128)}, f32[256,128]{1,0:T(8,128)S(1)}, u32[]{:S(2)}, u32[]{:S(2)}) %collective-permute-start) | collective-permute-done | bytes 131104 | tf_op jit(solution)/shard_map/ppermute | solution.py:344
  105.4 0.7 copy-done.6
  106.1 13.0 %all-to-all-start.2 = ((f32[32,24,1024]{2,1,0:T(8,128)}), f32[32,24,1024]{2,1,0:T(8,128)}, u32[]{:S(2)}, u32[]{:S(2)}) async-start(f32[32,24,1024]{2,1,0:T(8,128)} %bitcast.6), calls=%async_computation.2 | async-start | bytes 6291456 | tf_op jit(solution)/shard_map/all_to_all | solution.py:315
  119.1 96.4 %all-gather.11.cloned.1.call-done = f32[8192,64]{1,0:T(8,128)} async-done(((f32[32,64]{1,0:T(8,128)}), f32[8192,64]{1,0:T(8,128)}) %all-gather.11.cloned.1.call-update) | async-done | bytes 2097168 | tf_op jit(solution)/shard_map/all_gather | solution.py:335
  215.5 1.6 slice-done
  217.1 0.6 copy.6
  217.7 2.7 slice.11
  220.5 6.1 %copy.7 = f32[16,32,2,8,32]{4,3,2,1,0:T(8,128)} copy(f32[16,32,2,8,32]{1,3,0,4,2:T(8,128)} %bitcast.23) | data formatting | bytes 2097152 | tf_op jit(solution)/shard_map/transpose | solution.py:336
  226.6 3.5 %reshape.29.s_ref = f32[512,512]{1,0:T(8,128)S(1)} reshape(f32[16,32,2,8,32]{4,3,2,1,0:T(8,128)} %copy.7) | data formatting | bytes 2097152 | tf_op jit(solution)/shard_map/reshape | solution.py:336
  230.1 53.3 %factor.1 = (f32[512,512]{1,0:T(8,128)S(1)}, f32[512,512]{1,0:T(8,128)S(1)}) custom-call(f32[512,512]{1,0:T(8,128)S(1)} %reshape.29.s_ref), custom_call_target="tpu_custom_call" | custom-call | flops 30000001024 | bytes 100000000 | tf_op jit(solution)/shard_map/factor/pallas_call | solution.py:347
  283.5 1.0 copy-done.2
  284.5 0.6 constant_dynamic-slice_fusion.low_ref
  285.1 23.5 %all-gather.9.cloned.1.call-done = f32[8192,128]{1,0:T(8,128)} async-done(((f32[256,128]{1,0:T(8,128)}), f32[8192,128]{1,0:T(8,128)}) %all-gather.9.cloned.1.call-update) | async-done | bytes 4194320 | tf_op jit(solution)/shard_map/all_gather | solution.py:345
  308.6 24.9 %final.1 = f32[512,2048]{1,0:T(8,128)} custom-call(s32[2]{0:T(128)} %copy-done.5, s32[2,32,16]{2,1,0:T(8,128)} %copy-done.4, s32[2,1,2048]{2,1,0:T(1,128)} %copy-done.3, f32[2,384,1024]{2,1,0:T(8,128)} %bitcast.7.x_ref, f32[512,2048]{1,0:T(8,128)} %front_ref.3, f32[8,256,128]{2,1,0:T(8,128)} %bitcast.25, f32[32,256,128]{2,1,0:T(8,128)} %bitcast.24, ...), custom_call_target="tpu_custom_call" | custom-call | tf_op jit(solution)/shard_map/final/pallas_call | solution.py:361
  (21 shorter events, 0.2 us)
Async XLA Ops:
  7.4 1.6 copy-start.1
  9.0 11.9 %copy-start.7 = (s32[2,8192]{1,0:T(2,128)S(1)}, s32[2,8192]{1,0:T(2,128)}, u32[]{:S(2)}) copy-start(s32[2,8192]{1,0:T(2,128)} %param.5) | copy-start | bytes 196612
  13.7 53.0 %all-to-all-start = ((f32[8,512,128]{2,1,0:T(8,128)}), f32[8,512,128]{2,1,0:T(8,128)S(1)}, u32[]{:S(2)}, u32[]{:S(2)}) async-start(f32[8,512,128]{2,1,0:T(8,128)} %columns.1), calls=%async_computation | async-start | bytes 4194304 | tf_op jit(solution)/shard_map/all_to_all | solution.py:284
  70.4 16.4 %all-to-all-start.1 = ((f32[32,24,128]{2,1,0:T(8,128)}), f32[32,24,128]{2,1,0:T(8,128)S(1)}, u32[]{:S(2)}, u32[]{:S(2)}) async-start(f32[32,24,128]{2,1,0:T(8,128)} %bitcast.5), calls=%async_computation.1 | async-start | bytes 786432 | tf_op jit(solution)/shard_map/all_to_all | solution.py:311
  78.0 137.5 %all-gather.11.cloned.1.call-start = ((), (), s32[]{:S(2)}) async-start(), calls=%async_computation.5 | async-start | bytes 4210688 | tf_op jit(solution)/shard_map/all_gather | solution.py:335
  78.2 27.9 %copy-start.5 = (s32[2]{0:T(128)}, s32[2]{0:T(128)S(1)}, u32[]{:S(2)}) copy-start(s32[2]{0:T(128)S(1)} %pad_add_fusion.at_ref) | copy-start | bytes 28
  80.6 25.6 %copy-start.4 = (s32[2,32,16]{2,1,0:T(8,128)}, s32[2,32,16]{2,1,0:T(8,128)S(1)}, u32[]{:S(2)}) copy-start(s32[2,32,16]{2,1,0:T(8,128)S(1)} %get-tuple-element.13.slot_ref) | copy-start | bytes 12292
  80.7 25.5 %copy-start.3 = (s32[2,1,2048]{2,1,0:T(1,128)}, s32[2,1,2048]{2,1,0:T(1,128)S(1)}, u32[]{:S(2)}) copy-start(s32[2,1,2048]{2,1,0:T(1,128)S(1)} %reshape.35.col_ref) | copy-start | bytes 49156
  86.8 2.2 copy-start
  92.6 192.5 %all-gather.7.cloned.1.call-start = ((), (), s32[]{:S(2)}) async-start(), calls=%async_computation.3 | async-start | bytes 1179648 | tf_op jit(solution)/shard_map/all_gather | solution.py:337
  93.4 215.2 %all-gather.9.cloned.1.call-start = ((), (), s32[]{:S(2)}) async-start(), calls=%async_computation.4 | async-start | bytes 4325376 | tf_op jit(solution)/shard_map/all_gather | solution.py:345
  93.4 12.0 %collective-permute-start = (f32[256,128]{1,0:T(8,128)}, f32[256,128]{1,0:T(8,128)S(1)}, u32[]{:S(2)}, u32[]{:S(2)}) collective-permute-start(f32[256,128]{1,0:T(8,128)} %panel.1), channel_id=1, source_target_pairs={{0,0},{1,8},{2,16},{3,24},{4,32},{5,40},{6,48},{7,56},{8,1},{9,9},... | collective-permute-start | bytes 393224 | tf_op jit(solution)/shard_map/ppermute | solution.py:344
  105.4 0.7 copy-start.6
  106.1 179.0 %all-to-all-start.2 = ((f32[32,24,1024]{2,1,0:T(8,128)}), f32[32,24,1024]{2,1,0:T(8,128)}, u32[]{:S(2)}, u32[]{:S(2)}) async-start(f32[32,24,1024]{2,1,0:T(8,128)} %bitcast.6), calls=%async_computation.2 | async-start | bytes 6291456 | tf_op jit(solution)/shard_map/all_to_all | solution.py:315
  215.5 1.6 slice-start
  283.4 1.0 copy-start.2
Sparse Core Ops, SparseCore 0:
  92.7 122.7 all-gather.10
  217.3 37.0 all-gather.6
  257.0 51.5 all-gather.8

commit v2 on v1

--- a/solution.py
+++ b/solution.py
@@ -67,7 +67,7 @@
         o_ref[2 * pair + 1] = out[:, 128:]
 
 
-def rows_kernel(map_ref, x_ref, o_ref, p_ref):
+def rows_kernel(map_ref, x_ref, o_ref):
     owner = (map_ref[...] >> 5) & 31
     slot = owner * CAP + ranks_of(owner, 32, 32)
     n = owner.shape[1]
@@ -76,8 +76,6 @@
         high, low = split(jnp.concatenate([x_ref[2 * pair], x_ref[2 * pair + 1]], axis=1))
         out = mm(pick, high) + mm(pick, low)
         o_ref[:, pl.ds(pair * 256, 256)] = out
-        if pair == 0:
-            p_ref[...] = out[:, :128]
 
 
 def index_kernel(at_ref, map_ref, slot_ref, col_ref):
@@ -122,23 +120,6 @@
     return jnp.concatenate(parts, axis=0)
 
 
-def panel_kernel(at_ref, slot_ref, col_ref, x_ref, front_ref, o_ref):
-    rg, cg = at_ref[0], at_ref[1]
-    total = jnp.where(natural_lower(rg, cg, 512, 128, 0), front_ref[...], F32(0.0))
-    n = x_ref.shape[1]
-    for child in range(2):
-        pick = row_picker(slot_ref[child], n)
-        high, low = split(x_ref[child])
-        high, low = split(mm(pick, high) + mm(pick, low))
-        put = onehot(col_ref[child] == iota((128, 128), 0))
-        total = total + mm(high, put) + mm(low, put)
-    left = iota((64, 128), 1) < 64
-    for t in range(4):
-        a = total[t * 128 : t * 128 + 64]
-        b = total[t * 128 + 64 : t * 128 + 128]
-        o_ref[t * 64 : t * 64 + 64, :] = jnp.where(left, a, pltpu.roll(b, 64, 1))
-
-
 def sweep(w):
     tiles = [w[8 * i : 8 * i + 8, :] for i in range(16)]
     lane = iota((8, 128), 1)
@@ -169,10 +150,205 @@
     )
 
 
-def factor_kernel(s_ref, low_ref, inv_ref, w_ref):
+def remote(src, dst, send, recv, device):
+    return pltpu.make_async_remote_copy(
+        src_ref=src, dst_ref=dst, send_sem=send, recv_sem=recv, device_id=device,
+        device_id_type=pl.DeviceIdType.MESH,
+    )
+
+
+def panel_kernel(
+    cmap_ref, rmap_ref, slot_ref, child_ref, front_ref,
+    low_ref, inv_ref, own_ref, cols_ref,
+    pan_send, pan_recv, rows_send, rows_recv, piece, swapped, head_send, head_recv, sbuf, w_ref,
+    pan_s, pan_r, row_s, row_r, head_s, head_r, own_s, own_r, swap_s, swap_r, piv_s, piv_r,
+    fan_s, fan_r, pass_s, loc_s,
+):
+    sub, row, cg = lax.axis_index("sub"), lax.axis_index("row"), lax.axis_index("col")
+    rg = sub * 16 + row
+    quarter, place = rg // 8, rg % 8
+    mate = quarter * 8 + cg
+    mate_id = (mate // 16, mate % 16, place)
+    moves = place != cg
+    twin = (1 - sub, row, cg)
+
+    def each(first, last, fn):
+        def go(q, carry):
+            fn(q)
+            return carry
+
+        lax.fori_loop(first, last, go, 0)
+
+    def line(q):
+        return (cg + q) % 8
+
+    def plane(q):
+        p = (rg + q) % 32
+        return p, (p // 16, p % 16, cg)
+
+    def chip(q):
+        r = (row + q) % 16
+        return r, (sub, r, cg)
+
+    barrier = pltpu.get_barrier_semaphore()
+
+    def greet(device):
+        pl.semaphore_signal(barrier, inc=1, device_id=device, device_id_type=pl.DeviceIdType.MESH)
+
+    each(1, 8, lambda q: greet((sub, row, line(q))))
+    each(1, 32, lambda q: greet(plane(q)[1]))
+
+    @pl.when(moves)
+    def _():
+        greet(mate_id)
+
+    pl.semaphore_wait(barrier, jnp.where(moves, 39, 38))
+
+    pan_recv[64:, :] = jnp.zeros((64, 512), F32)
+
+    def to_line(q):
+        return remote(
+            pan_send.at[q], pan_recv.at[pl.ds(0, 64)], pan_s.at[q], pan_r, (sub, row, q)
+        )
+
+    @pl.when(cg == 0)
+    def _():
+        keep = row * 512 + iota((512, 512), 0) >= iota((512, 512), 1)
+        high, low = split(jnp.where(keep, child_ref[...], F32(0.0)))
+        for q in range(7, -1, -1):
+            n = iota((64, 512), 0)
+            nat = ((n >> 5) * 8 + q) * NB + (n & 31)
+            pick = onehot(cmap_ref[...] == nat)
+            out = mt(pick, high) + mt(pick, low)
+            if q == 0:
+                pan_recv[:64, :] = out
+            else:
+                pan_send[q] = out
+                to_line(q).start()
+
+    owner = (rmap_ref[...] >> 5) & 31
+    slot = owner * CAP + ranks_of(owner, 32, 32)
+    pick_rows = onehot(slot == iota((32 * CAP, 512), 0))
+
+    @pl.when(cg != 0)
+    def _():
+        to_line(cg).wait_recv()
+
+    high, low = split(pan_recv[...])
+    out = mt(pick_rows, high) + mt(pick_rows, low)
+    for p in range(32):
+        rows_send[p] = out[p * CAP : p * CAP + CAP, :]
+
+    def to_plane(q):
+        p, device = plane(q)
+        return remote(rows_send.at[p], rows_recv.at[rg], row_s.at[p], row_r.at[rg], device)
+
+    def from_plane(q):
+        p, device = plane(q)
+        return remote(rows_send.at[p], rows_recv.at[p], row_s.at[p], row_r.at[p], device)
+
+    each(1, 32, lambda q: to_plane(q).start())
+    rows_recv[rg] = rows_send[rg]
+    total = jnp.where(natural_lower(rg, cg, 512, 128, 0), front_ref[...], F32(0.0))
+    picks = [row_picker(slot_ref[child], 16 * CAP) for child in range(2)]
+    each(1, 32, lambda q: from_plane(q).wait_recv())
+    for child in range(2):
+        got = rows_recv[child * 16 : child * 16 + 16].reshape(16 * CAP, 128)
+        high, low = split(got)
+        total = total + mm(picks[child], high) + mm(picks[child], low)
+    left = iota((64, 128), 1) < 64
+    for t in range(4):
+        a = total[t * 128 : t * 128 + 64]
+        b = total[t * 128 + 64 : t * 128 + 128]
+        piece[t * 64 : t * 64 + 64, :] = jnp.where(left, a, pltpu.roll(b, 64, 1))
+    head_send[...] = total[:NB, :]
+
+    def head(q, at):
+        return remote(
+            head_send, head_recv.at[at], head_s.at[q], head_r.at[at], (sub, row, line(q))
+        )
+
+    def swap():
+        return remote(piece, swapped, swap_s, swap_r, mate_id)
+
+    def own(q, at):
+        return remote(piece, own_ref.at[at], own_s.at[q], own_r.at[at], (sub, row, line(q)))
+
+    own_local = pltpu.make_async_copy(piece, own_ref.at[cg], loc_s.at[0])
+
+    @pl.when(sub == 0)
+    def _():
+        each(1, 8, lambda q: head(q, cg).start())
+
+    @pl.when(moves)
+    def _():
+        swap().start()
+
+    head_recv[cg] = head_send[...]
+
+    def pivot(q, at):
+        return remote(sbuf.at[at], sbuf.at[at], piv_s.at[q], piv_r.at[at], chip(q)[1])
+
+    def pivot_twin(at):
+        return remote(sbuf.at[at], sbuf.at[at], piv_s.at[16 + at], piv_r.at[at], (1, row, cg))
+
+    @pl.when(sub == 0)
+    def _():
+        each(1, 8, lambda q: head(q, line(q)).wait_recv())
+        half = iota((NB, 128), 1) < 64
+        rows = [
+            jnp.where(half, head_recv[2 * p], pltpu.roll(head_recv[2 * p + 1], 64, 1))
+            for p in range(4)
+        ]
+        sbuf[row] = jnp.concatenate(rows, axis=1)
+        each(1, 16, lambda q: pivot(q, row).start())
+        pivot_twin(row).start()
+
+    @pl.when(moves)
+    def _():
+        swap().wait_recv()
+
+    @pl.when(jnp.logical_not(moves))
+    def _():
+        swapped[...] = piece[...]
+
+    def fan(q, at):
+        return remote(swapped, cols_ref.at[at], fan_s.at[q], fan_r.at[at], chip(q)[1])
+
+    def hand(at, src):
+        return remote(src, cols_ref.at[at], pass_s.at[at % 16], fan_r.at[at], twin)
+
+    def twin_hand(at):
+        return remote(swapped, cols_ref.at[at], pass_s.at[at % 16], fan_r.at[at], twin)
+
+    cols_local = pltpu.make_async_copy(swapped, cols_ref.at[rg], loc_s.at[1])
+    each(1, 16, lambda q: fan(q, rg).start())
+    hand(rg, swapped).start()
+    cols_local.start()
+    each(1, 8, lambda q: own(q, cg).start())
+    own_local.start()
+
+    @pl.when(sub == 0)
+    def _():
+        def relay(q):
+            at = chip(q)[0]
+            pivot(q, at).wait_recv()
+            pivot_twin(at).start()
+
+        each(1, 16, relay)
+
+    @pl.when(sub == 1)
+    def _():
+        each(0, 16, lambda q: pivot_twin(q).wait_recv())
+
+    turned = sbuf[...].reshape(PW, PW).T
+    for c8 in range(8):
+        for half in range(2):
+            src = (c8 * 2 + half) * NB
+            w_ref[(half * 8 + c8) * NB : (half * 8 + c8 + 1) * NB, :PW] = turned[src : src + NB, :]
     r, c = iota((PW, PW), 0), iota((PW, PW), 1)
-    raw = s_ref[...]
-    w_ref[:, :PW] = jnp.where(r >= c, raw, F32(0.0)) + jnp.where(r > c, raw, F32(0.0)).T
+    raw = w_ref[:, :PW]
+    w_ref[:, :PW] = jnp.where(c >= r, raw, F32(0.0)) + jnp.where(c > r, raw, F32(0.0)).T
     w_ref[:, PW:] = jnp.where(r == c, F32(1.0), F32(0.0))
 
     def step(kb, carry):
@@ -184,6 +360,15 @@
         w_ref[...] = w_ref[...] - exact(ahead, rows, ((0,), (0,)))
         w_ref[pl.ds(at, 128), :] = jnp.concatenate([ahead, rows[:, PW:]], axis=1)
         w_ref[pl.ds(at, 128), pl.ds(at, 128)] = upper
+
+        def relay(q):
+            @pl.when(q < 16)
+            def _():
+                r = chip(q)[0]
+                fan(q, sub * 16 + r).wait_recv()
+                hand(sub * 16 + r, cols_ref.at[sub * 16 + r]).start()
+
+        each(kb * 4 + 1, kb * 4 + 5, relay)
         return carry
 
     lax.fori_loop(0, PW // 128, step, 0)
@@ -193,6 +378,29 @@
         for half in range(2):
             src = (half * 8 + c8) * NB
             inv_ref[(c8 * 2 + half) * NB : (c8 * 2 + half + 1) * NB, :] = turned[src : src + NB, :]
+
+    each(0, 16, lambda q: twin_hand((1 - sub) * 16 + q).wait_recv())
+    each(0, 16, lambda q: twin_hand(sub * 16 + q).wait_send())
+    each(1, 16, lambda q: fan(q, rg).wait_send())
+    each(1, 8, lambda q: own(q, line(q)).wait_recv())
+    each(1, 8, lambda q: own(q, cg).wait_send())
+    own_local.wait()
+    cols_local.wait()
+    each(1, 32, lambda q: to_plane(q).wait_send())
+
+    @pl.when(cg == 0)
+    def _():
+        each(1, 8, lambda q: to_line(q).wait_send())
+
+    @pl.when(moves)
+    def _():
+        swap().wait_send()
+
+    @pl.when(sub == 0)
+    def _():
+        each(1, 8, lambda q: head(q, cg).wait_send())
+        each(1, 16, lambda q: pivot(q, row).wait_send())
+        each(0, 16, lambda q: pivot_twin(q).wait_send())
 
 
 def unpack(pieces, left):
@@ -297,66 +505,61 @@
     )(at, child_map.reshape(2, 16, 512))
     cols = cols.reshape(2, 1, 2048)
 
-    packed, packed_panel = pl.pallas_call(
+    DMA = pltpu.SemaphoreType.DMA
+    lower, inverse, own_rows, col_rows = pl.pallas_call(
+        panel_kernel,
+        out_shape=(
+            jax.ShapeDtypeStruct((PW, PW), F32),
+            jax.ShapeDtypeStruct((PW, PW), F32),
+            jax.ShapeDtypeStruct((8, 256, 128), F32),
+            jax.ShapeDtypeStruct((32, 256, 128), F32),
+        ),
+        grid=(1,),
+        in_specs=[
+            pl.BlockSpec((1, 512), lambda i: (0, 0)),
+            pl.BlockSpec((1, 512), lambda i: (0, 0)),
+            pl.BlockSpec((2, NB, 16), lambda i: (0, 0, 0)),
+            pl.BlockSpec((512, 512), lambda i: (0, 0)),
+            pl.BlockSpec((512, 128), lambda i: (0, 0)),
+        ],
+        out_specs=(
+            pl.BlockSpec((PW, PW), lambda i: (0, 0)),
+            pl.BlockSpec((PW, PW), lambda i: (0, 0)),
+            pl.BlockSpec(memory_space=pl.ANY),
+            pl.BlockSpec(memory_space=pl.ANY),
+        ),
+        scratch_shapes=[
+            pltpu.VMEM((8, 64, 512), F32),
+            pltpu.VMEM((128, 512), F32),
+            pltpu.VMEM((32, CAP, 128), F32),
+            pltpu.VMEM((32, CAP, 128), F32),
+            pltpu.VMEM((256, 128), F32),
+            pltpu.VMEM((256, 128), F32),
+            pltpu.VMEM((NB, 128), F32),
+            pltpu.VMEM((8, NB, 128), F32),
+            pltpu.VMEM((16, NB, PW), F32),
+            pltpu.VMEM((PW, 2 * PW), F32),
+            DMA((8,)), DMA, DMA((32,)), DMA((32,)), DMA((8,)), DMA((8,)), DMA((8,)), DMA((8,)),
+            DMA, DMA, DMA((32,)), DMA((16,)), DMA((16,)), DMA((32,)), DMA((16,)), DMA((2,)),
+        ],
+        name="panel",
+        compiler_params=pltpu.CompilerParams(
+            collective_id=1, has_side_effects=True, vmem_limit_bytes=40 << 20
+        ),
+        cost_estimate=pl.CostEstimate(flops=3 * 10**10, bytes_accessed=10**8, transcendentals=0),
+    )(own_map[:, :512], row_targets, slots, child_blocks[0], front)
+
+    packed = pl.pallas_call(
         rows_kernel,
-        out_shape=(
-            jax.ShapeDtypeStruct((32 * CAP, 1024), F32),
-            jax.ShapeDtypeStruct((32 * CAP, 128), F32),
-        ),
+        out_shape=jax.ShapeDtypeStruct((32 * CAP, 1024), F32),
         in_specs=[VM, VM],
-        out_specs=(VM, VM),
+        out_specs=VM,
         name="rows",
         compiler_params=params(40),
     )(row_targets, moved)
-    got_panel = lax.all_to_all(
-        packed_panel.reshape(32, CAP, 128), ("sub", "row"), split_axis=0, concat_axis=0, tiled=True
-    )
-    packed, got_panel = lax.optimization_barrier((packed, got_panel))
     received = lax.all_to_all(
         packed.reshape(32, CAP, 1024), ("sub", "row"), split_axis=0, concat_axis=0, tiled=True
     )
-
-    piece = pl.pallas_call(
-        panel_kernel,
-        out_shape=jax.ShapeDtypeStruct((256, 128), F32),
-        grid=(1,),
-        in_specs=[
-            SM,
-            pl.BlockSpec((2, NB, 16), lambda i: (0, 0, 0)),
-            pl.BlockSpec((2, 1, 128), lambda i: (0, 0, 0)),
-            pl.BlockSpec((2, 16 * CAP, 128), lambda i: (0, 0, 0)),
-            pl.BlockSpec((512, 128), lambda i: (0, 0)),
-        ],
-        out_specs=pl.BlockSpec((256, 128), lambda i: (0, 0)),
-        name="panel",
-        compiler_params=params(40),
-    )(at, slots, cols, got_panel.reshape(2, 16 * CAP, 128), front)
-
-    head = lax.all_gather(piece[:NB, :64], AXES, axis=0)
-    head = head.reshape(32, 8, NB, 2, NB)[:16].transpose(0, 2, 3, 1, 4).reshape(PW, PW)
-    own_rows = lax.all_gather(piece, "col", axis=0)
-    swaps = [
-        ((8 * i + a) * 8 + b, (8 * i + b) * 8 + a)
-        for i in range(4)
-        for a in range(8)
-        for b in range(8)
-    ]
-    swapped = lax.ppermute(piece, AXES, swaps)
-    col_rows = lax.all_gather(swapped, ("sub", "row"), axis=0)
-
-    lower, inverse = pl.pallas_call(
-        factor_kernel,
-        out_shape=(
-            jax.ShapeDtypeStruct((PW, PW), F32),
-            jax.ShapeDtypeStruct((PW, PW), F32),
-        ),
-        in_specs=[VM],
-        out_specs=(VM, VM),
-        scratch_shapes=[pltpu.VMEM((PW, 2 * PW), F32)],
-        name="factor",
-        compiler_params=params(40),
-        cost_estimate=pl.CostEstimate(flops=3 * 10**10, bytes_accessed=10**8, transcendentals=0),
-    )(head)
 
     return pl.pallas_call(
         final_kernel,

time: 344 us -> 249 us (0.72)
  the two profiles are of different devices: /device:TPU:132 before, /device:TPU:10 now
where the time goes in v2:
time: 249 us; the launch traced here: 248 us
  Pallas kernels  169 us (68%)
  waiting for transfers between devices  51.1 us (21%)
  starting transfers between devices  16.3 us (7%)
  local copies, waits for them, and re-layouts  11.4 us (5%)
    pallas_call x1, Pallas kernels, body(): pl.pallas_call(panel_kernel, out_shape=(jax.ShapeDtypeStruct((PW, PW), F3...  135 us
    all_to_all x1, waiting for transfers between devices, body(): lax.all_to_all(by_column, 'col', split_axis=0, concat_axis=0, tiled=True)  51.1 us
    pallas_call x1, Pallas kernels, body(): pl.pallas_call(final_kernel, out_shape=jax.ShapeDtypeStruct((512, 2048),...  25 us
    unnamed x21, local copies, waits for them, and re-layouts  9.19 us
    all_to_all x1, starting transfers between devices, body(): lax.all_to_all(by_column, 'col', split_axis=0, concat_axis=0, tiled=True)  8.61 us
    all_to_all x1, starting transfers between devices, body(): lax.all_to_all(packed.reshape(32, CAP, 1024), ('sub', 'row'), split_axis=...  7.69 us
  transfers between devices with their start and end apart: 2, of which 1 were waited for; matrix products, arithmetic and copies ran while one was open for 1% of the time, Pallas kernels for 55%

profile of v2, /device:TPU:10, one launch (start us, length us, event | category | flops | bytes accessed | tf_op | source)
XLA Modules:
  0.0 248.2 jit_solution(11061066262931769839)
XLA Ops:
  0.0 0.1 pad_add_fusion.1.at_ref
  0.1 0.8 dynamic_slice.14.map_ref
  0.9 0.0 copy-start.3
  0.9 1.6 copy-done.3
  2.4 3.4 %columns.1 = f32[8,512,128]{2,1,0:T(8,128)S(1)} custom-call(s32[2]{0:T(128)S(1)} %pad_add_fusion.1.at_ref, s32[1,1024]{1,0:T(1,128)S(1)} %dynamic_slice.14.map_ref, f32[512,1024]{1,0:T(8,128)S(1)} %bitcast.11), custom_call_target="tpu_custom_call" | custom-call | tf_op jit(solution)/shard_map/columns/pallas_call | solution.py:484
  5.8 0.0 copy-start
  5.8 1.3 copy-done
  7.1 0.0 copy-start.9
  7.1 8.6 %all-to-all-start = ((f32[8,512,128]{2,1,0:T(8,128)}), f32[8,512,128]{2,1,0:T(8,128)S(1)}, u32[]{:S(2)}, u32[]{:S(2)}) async-start(f32[8,512,128]{2,1,0:T(8,128)} %copy-done), calls=%async_computation | async-start | bytes 4194304 | tf_op jit(solution)/shard_map/all_to_all | solution.py:492
  15.7 0.0 copy-done.9
  15.8 0.1 constant_dynamic-slice_fusion.1
  15.8 51.1 %all-to-all-done.x_ref = f32[8,512,128]{2,1,0:T(8,128)S(1)} async-done(((f32[8,512,128]{2,1,0:T(8,128)}), f32[8,512,128]{2,1,0:T(8,128)S(1)}, u32[]{:S(2)}, u32[]{:S(2)}) %all-to-all-start) | async-done | bytes 2097184 | tf_op jit(solution)/shard_map/all_to_all | solution.py:492
  66.9 3.7 %rows.1 = f32[768,1024]{1,0:T(8,128)} custom-call(s32[1,512]{1,0:T(1,128)S(1)} %get-tuple-element.18.map_ref.rmap_ref, f32[8,512,128]{2,1,0:T(8,128)S(1)} %all-to-all-done.x_ref), custom_call_target="tpu_custom_call" | custom-call | tf_op jit(solution)/shard_map/rows/pallas_call | solution.py:552
  70.6 0.0 copy-start.4
  70.6 7.7 %all-to-all-start.1 = ((f32[32,24,1024]{2,1,0:T(8,128)}), f32[32,24,1024]{2,1,0:T(8,128)}, u32[]{:S(2)}, u32[]{:S(2)}) async-start(f32[32,24,1024]{2,1,0:T(8,128)} %bitcast.5), calls=%async_computation.1 | async-start | bytes 6291456 | tf_op jit(solution)/shard_map/all_to_all | solution.py:560
  78.3 0.1 pad_add_fusion.at_ref
  78.4 2.4 index.1
  80.8 0.0 copy-start.7
  80.8 0.7 reshape.16.col_ref
  81.5 0.0 copy-done.4
  81.5 0.0 copy-start.1
  81.5 2.2 copy-done.1
  83.7 134.8 %panel.1 = (f32[512,512]{1,0:T(8,128)S(1)}, f32[512,512]{1,0:T(8,128)S(1)}, f32[8,256,128]{2,1,0:T(8,128)S(1)}, f32[32,256,128]{2,1,0:T(8,128)S(1)}) custom-call(s32[1,512]{1,0:T(1,128)S(1)} %get-tuple-element.17.cmap_ref, s32[1,512]{1,0:T(1,128)S(1)} %get-tuple-element.18.map_ref.rmap_ref, s32[2,32,16]{2,1,0:T(8,128)S(1)} %get-tuple-element.11.slot_ref, ...), custom_call_target="tpu_custom_call" | custom-call | flops 30000001024 | bytes 100000000 | tf_op jit(solution)/shard_map/panel/pallas_call | solution.py:509
  218.5 0.0 copy-done.8
  218.5 0.0 copy-done.7
  218.5 0.0 copy-start.2
  218.5 2.0 copy-done.2
  220.5 1.1 copy-done.5
  221.6 1.0 copy-done.6
  222.6 0.6 constant_dynamic-slice_fusion.low_ref
  223.2 0.0 all-to-all-done.1
  223.2 25.0 %final.1 = f32[512,2048]{1,0:T(8,128)} custom-call(s32[2]{0:T(128)} %copy-done.8, s32[2,32,16]{2,1,0:T(8,128)} %copy-done.7, s32[2,1,2048]{2,1,0:T(1,128)} %reshape.16.col_ref, f32[2,384,1024]{2,1,0:T(8,128)} %bitcast.6.x_ref, f32[512,2048]{1,0:T(8,128)} %front_ref.3, f32[8,256,128]{2,1,0:T(8,128)} %copy-done.6, f32[32,256,128]{2,1,0:T(8,128)} %copy-done.2, ...), custom_call_target="tpu_custom_call" | custom-call | tf_op jit(solution)/shard_map/final/pallas_call | solution.py:564
  (4 shorter events, 0.0 us)
Async XLA Ops:
  0.9 1.6 copy-start.3
  5.8 1.3 copy-start
  7.1 8.6 %copy-start.9 = (s32[2,8192]{1,0:T(2,128)S(1)}, s32[2,8192]{1,0:T(2,128)}, u32[]{:S(2)}) copy-start(s32[2,8192]{1,0:T(2,128)} %param.5) | copy-start | bytes 196612
  7.1 59.8 %all-to-all-start = ((f32[8,512,128]{2,1,0:T(8,128)}), f32[8,512,128]{2,1,0:T(8,128)S(1)}, u32[]{:S(2)}, u32[]{:S(2)}) async-start(f32[8,512,128]{2,1,0:T(8,128)} %copy-done), calls=%async_computation | async-start | bytes 4194304 | tf_op jit(solution)/shard_map/all_to_all | solution.py:492
  70.6 10.9 %copy-start.4 = (f32[1,512,1024]{2,1,0:T(8,128)S(1)}, f32[1,512,1024]{2,1,0:T(8,128)}, u32[]{:S(2)}) copy-start(f32[1,512,1024]{2,1,0:T(8,128)} %param.4) | copy-start | bytes 6291460
  70.6 152.6 %all-to-all-start.1 = ((f32[32,24,1024]{2,1,0:T(8,128)}), f32[32,24,1024]{2,1,0:T(8,128)}, u32[]{:S(2)}, u32[]{:S(2)}) async-start(f32[32,24,1024]{2,1,0:T(8,128)} %bitcast.5), calls=%async_computation.1 | async-start | bytes 6291456 | tf_op jit(solution)/shard_map/all_to_all | solution.py:560
  78.4 140.1 %copy-start.8 = (s32[2]{0:T(128)}, s32[2]{0:T(128)S(1)}, u32[]{:S(2)}) copy-start(s32[2]{0:T(128)S(1)} %pad_add_fusion.at_ref) | copy-start | bytes 28
  80.8 137.7 %copy-start.7 = (s32[2,32,16]{2,1,0:T(8,128)}, s32[2,32,16]{2,1,0:T(8,128)S(1)}, u32[]{:S(2)}) copy-start(s32[2,32,16]{2,1,0:T(8,128)S(1)} %get-tuple-element.11.slot_ref) | copy-start | bytes 12292
  81.5 2.2 copy-start.1
  218.5 2.0 copy-start.2
  220.5 1.1 copy-start.5
  221.6 1.0 copy-start.6

commit v3 on v2

--- a/solution.py
+++ b/solution.py
@@ -53,33 +53,7 @@
     return (jnp.sum(counts * member, axis=0, keepdims=True) - 1.0).astype(I32)
 
 
-def columns_kernel(at_ref, map_ref, x_ref, o_ref):
-    rows, cols = x_ref.shape
-    row0, col0 = at_ref[0], at_ref[1]
-    keep = row0 + iota((rows, cols), 0) >= col0 + iota((rows, cols), 1)
-    high, low = split(jnp.where(keep, x_ref[...], F32(0.0)))
-    owner = (map_ref[...] >> 5) & 7
-    slot = owner * 128 + ranks_of(owner, 8, 16)
-    for pair in range(4):
-        pick = onehot(slot == pair * 256 + iota((256, cols), 0))
-        out = mt(high, pick) + mt(low, pick)
-        o_ref[2 * pair] = out[:, :128]
-        o_ref[2 * pair + 1] = out[:, 128:]
-
-
-def rows_kernel(map_ref, x_ref, o_ref):
-    owner = (map_ref[...] >> 5) & 31
-    slot = owner * CAP + ranks_of(owner, 32, 32)
-    n = owner.shape[1]
-    pick = onehot(slot == iota((32 * CAP, n), 0))
-    for pair in range(4):
-        high, low = split(jnp.concatenate([x_ref[2 * pair], x_ref[2 * pair + 1]], axis=1))
-        out = mm(pick, high) + mm(pick, low)
-        o_ref[:, pl.ds(pair * 256, 256)] = out
-
-
-def index_kernel(at_ref, map_ref, slot_ref, col_ref):
-    rg, cg = at_ref[0], at_ref[1]
+def index_work(rg, cg, map_ref, slot_ref, col_ref):
     upto = onehot(iota((512, 512), 0) <= iota((512, 512), 1))
     before64 = onehot(iota((64, 64), 1) < iota((64, 64), 0))
     before32 = onehot(iota((32, 32), 0) < iota((32, 32), 1))
@@ -158,11 +132,11 @@
 
 
 def panel_kernel(
-    cmap_ref, rmap_ref, slot_ref, child_ref, front_ref,
-    low_ref, inv_ref, own_ref, cols_ref,
-    pan_send, pan_recv, rows_send, rows_recv, piece, swapped, head_send, head_recv, sbuf, w_ref,
+    cmap_ref, rmap_ref, map_ref, child_ref, front_ref,
+    low_ref, inv_ref, slot_ref, col_ref, own_ref, cols_ref, got_ref,
+    zsend, zrecv, xsend, pan_send, pan_recv, rows_send, rows_recv, piece, swapped, head_send, head_recv, sbuf, w_ref,
     pan_s, pan_r, row_s, row_r, head_s, head_r, own_s, own_r, swap_s, swap_r, piv_s, piv_r,
-    fan_s, fan_r, pass_s, loc_s,
+    fan_s, fan_r, pass_s, loc_s, z_s, z_r, x_s, x_r,
 ):
     sub, row, cg = lax.axis_index("sub"), lax.axis_index("row"), lax.axis_index("col")
     rg = sub * 16 + row
@@ -214,11 +188,11 @@
     @pl.when(cg == 0)
     def _():
         keep = row * 512 + iota((512, 512), 0) >= iota((512, 512), 1)
-        high, low = split(jnp.where(keep, child_ref[...], F32(0.0)))
+        high, low = split(jnp.where(keep, child_ref[:, :512], F32(0.0)))
         for q in range(7, -1, -1):
             n = iota((64, 512), 0)
             nat = ((n >> 5) * 8 + q) * NB + (n & 31)
-            pick = onehot(cmap_ref[...] == nat)
+            pick = onehot(cmap_ref[:, :512] == nat)
             out = mt(pick, high) + mt(pick, low)
             if q == 0:
                 pan_recv[:64, :] = out
@@ -226,9 +200,31 @@
                 pan_send[q] = out
                 to_line(q).start()
 
+    def bulk(h, q, at):
+        return remote(
+            zsend.at[h, q], zrecv.at[h, at], z_s.at[h, q], z_r.at[h, at], (sub, row, q)
+        )
+
+    keep = row * 512 + iota((512, 1024), 0) >= cg * 1024 + iota((512, 1024), 1)
+    high, low = split(jnp.where(keep, child_ref[...], F32(0.0)))
+    owner = (cmap_ref[...] >> 5) & 7
+    slot = owner * 128 + ranks_of(owner, 8, 16)
+
+    def bulk_half(h):
+        n = iota((512, 1024), 0)
+        pick = onehot(slot == (n >> 6) * 128 + h * 64 + (n & 63))
+        out = mt(pick, high) + mt(pick, low)
+        for q in range(8):
+            zsend[h, q] = out[q * 64 : q * 64 + 64, :]
+        zrecv[h, cg] = zsend[h, cg]
+
+    bulk_half(0)
+    each(1, 8, lambda q: bulk(0, line(q), cg).start())
+    bulk_half(1)
     owner = (rmap_ref[...] >> 5) & 31
     slot = owner * CAP + ranks_of(owner, 32, 32)
     pick_rows = onehot(slot == iota((32 * CAP, 512), 0))
+    index_work(rg, cg, map_ref, slot_ref, col_ref)
 
     @pl.when(cg != 0)
     def _():
@@ -285,6 +281,23 @@
         swap().start()
 
     head_recv[cg] = head_send[...]
+    each(1, 8, lambda q: bulk(1, line(q), cg).start())
+
+    def cross(h, q, at):
+        p, device = plane(q)
+        return remote(xsend.at[h, p], got_ref.at[h, at], x_s.at[h, p], x_r.at[h, at], device)
+
+    def keep_own(h):
+        return pltpu.make_async_copy(xsend.at[h, rg], got_ref.at[h, rg], loc_s.at[2 + h])
+
+    def cross_half(h):
+        each(1, 8, lambda q: bulk(h, line(q), line(q)).wait_recv())
+        high, low = split(zrecv[h].reshape(512, 512))
+        out = mt(pick_rows, high) + mt(pick_rows, low)
+        for p in range(32):
+            xsend[h, p] = out[p * CAP : p * CAP + CAP, :]
+        each(1, 32, lambda q: cross(h, q, rg).start())
+        keep_own(h).start()
 
     def pivot(q, at):
         return remote(sbuf.at[at], sbuf.at[at], piv_s.at[q], piv_r.at[at], chip(q)[1])
@@ -369,6 +382,11 @@
                 hand(sub * 16 + r, cols_ref.at[sub * 16 + r]).start()
 
         each(kb * 4 + 1, kb * 4 + 5, relay)
+
+        @pl.when(kb < 2)
+        def _():
+            cross_half(kb)
+
         return carry
 
     lax.fori_loop(0, PW // 128, step, 0)
@@ -387,6 +405,11 @@
     own_local.wait()
     cols_local.wait()
     each(1, 32, lambda q: to_plane(q).wait_send())
+    for h in range(2):
+        each(1, 8, lambda q: bulk(h, line(q), cg).wait_send())
+        each(1, 32, lambda q: cross(h, q, plane(q)[0]).wait_recv())
+        each(1, 32, lambda q: cross(h, q, rg).wait_send())
+        keep_own(h).wait()
 
     @pl.when(cg == 0)
     def _():
@@ -442,11 +465,13 @@
         nat = ((lane >> 5) * 8 + cg) * 32 + (lane & 31)
         pick = onehot((nat == iota((PW, 128), 0)) & (lane < 64))
         panel_ref[...] = mm(fh[...], pick) + mm(fl[...], pick)
-        n = x_ref.shape[1]
         for child in range(2):
-            pick = row_picker(slot_ref[child], n)
-            high, low = split(x_ref[child])
-            yh[child], yl[child] = split(mm(pick, high) + mm(pick, low))
+            pick = row_picker(slot_ref[child], 16 * CAP)
+            for h in range(2):
+                got = x_ref[h, child * 16 : child * 16 + 16].reshape(16 * CAP, 512)
+                high, low = split(got)
+                at = pl.ds(h * 512, 512)
+                yh[child, :, at], yl[child, :, at] = split(mm(pick, high) + mm(pick, low))
 
     inv = ih[...], il[...]
     parts = []
@@ -458,7 +483,9 @@
     )
     total = front_ref[...] - three((fh[...], fl[...]), split(cols), mt)
     for child in range(2):
-        put = onehot(col_ref[child] == iota((1024, 512), 0))
+        m = col_ref[child]
+        m = jnp.where(m < 0, -1, ((m >> 6) & 1) * 512 + (m >> 7) * 64 + (m & 63))
+        put = onehot(m == iota((1024, 512), 0))
         total = total + mm(yh[child], put) + mm(yl[child], put)
     total = jnp.where(natural_lower(rg, cg, 512, 512, ct * 512), total, F32(0.0))
     o_ref[...] = total
@@ -479,56 +506,40 @@
     own_map = lax.dynamic_index_in_dim(child_map, sub, 0, keepdims=True)
     row_targets = lax.dynamic_slice_in_dim(own_map, row * 512, 512, axis=1)
     col_targets = lax.dynamic_slice_in_dim(own_map, cg * 1024, 1024, axis=1)
-    start = jnp.stack([row * 512, cg * 1024]).astype(I32)
-
-    by_column = pl.pallas_call(
-        columns_kernel,
-        out_shape=jax.ShapeDtypeStruct((8, 512, 128), F32),
-        in_specs=[SM, VM, VM],
-        out_specs=VM,
-        name="columns",
-        compiler_params=params(40),
-    )(start, col_targets, child_blocks[0])
-    moved = lax.all_to_all(by_column, "col", split_axis=0, concat_axis=0, tiled=True)
-
-    slots, cols = pl.pallas_call(
-        index_kernel,
-        out_shape=(
-            jax.ShapeDtypeStruct((2, NB, 16), I32),
-            jax.ShapeDtypeStruct((2, 64, NB), I32),
-        ),
-        in_specs=[SM, VM],
-        out_specs=(VM, VM),
-        name="index",
-        compiler_params=params(40),
-        cost_estimate=pl.CostEstimate(flops=10**8, bytes_accessed=10**7, transcendentals=0),
-    )(at, child_map.reshape(2, 16, 512))
-    cols = cols.reshape(2, 1, 2048)
 
     DMA = pltpu.SemaphoreType.DMA
-    lower, inverse, own_rows, col_rows = pl.pallas_call(
+    lower, inverse, slots, cols, own_rows, col_rows, received = pl.pallas_call(
         panel_kernel,
         out_shape=(
             jax.ShapeDtypeStruct((PW, PW), F32),
             jax.ShapeDtypeStruct((PW, PW), F32),
+            jax.ShapeDtypeStruct((2, NB, 16), I32),
+            jax.ShapeDtypeStruct((2, 64, NB), I32),
             jax.ShapeDtypeStruct((8, 256, 128), F32),
             jax.ShapeDtypeStruct((32, 256, 128), F32),
+            jax.ShapeDtypeStruct((2, 32, CAP, 512), F32),
         ),
         grid=(1,),
         in_specs=[
+            pl.BlockSpec((1, 1024), lambda i: (0, 0)),
             pl.BlockSpec((1, 512), lambda i: (0, 0)),
-            pl.BlockSpec((1, 512), lambda i: (0, 0)),
-            pl.BlockSpec((2, NB, 16), lambda i: (0, 0, 0)),
-            pl.BlockSpec((512, 512), lambda i: (0, 0)),
+            pl.BlockSpec((2, 16, 512), lambda i: (0, 0, 0)),
+            pl.BlockSpec((512, 1024), lambda i: (0, 0)),
             pl.BlockSpec((512, 128), lambda i: (0, 0)),
         ],
         out_specs=(
             pl.BlockSpec((PW, PW), lambda i: (0, 0)),
             pl.BlockSpec((PW, PW), lambda i: (0, 0)),
+            pl.BlockSpec((2, NB, 16), lambda i: (0, 0, 0)),
+            pl.BlockSpec((2, 64, NB), lambda i: (0, 0, 0)),
+            pl.BlockSpec(memory_space=pl.ANY),
             pl.BlockSpec(memory_space=pl.ANY),
             pl.BlockSpec(memory_space=pl.ANY),
         ),
         scratch_shapes=[
+            pltpu.VMEM((2, 8, 64, 512), F32),
+            pltpu.VMEM((2, 8, 64, 512), F32),
+            pltpu.VMEM((2, 32, CAP, 512), F32),
             pltpu.VMEM((8, 64, 512), F32),
             pltpu.VMEM((128, 512), F32),
             pltpu.VMEM((32, CAP, 128), F32),
@@ -540,27 +551,17 @@
             pltpu.VMEM((16, NB, PW), F32),
             pltpu.VMEM((PW, 2 * PW), F32),
             DMA((8,)), DMA, DMA((32,)), DMA((32,)), DMA((8,)), DMA((8,)), DMA((8,)), DMA((8,)),
-            DMA, DMA, DMA((32,)), DMA((16,)), DMA((16,)), DMA((32,)), DMA((16,)), DMA((2,)),
+            DMA, DMA, DMA((32,)), DMA((16,)), DMA((16,)), DMA((32,)), DMA((16,)), DMA((4,)),
+            DMA((2, 8)), DMA((2, 8)), DMA((2, 32)), DMA((2, 32)),
         ],
         name="panel",
         compiler_params=pltpu.CompilerParams(
-            collective_id=1, has_side_effects=True, vmem_limit_bytes=40 << 20
+            collective_id=1, has_side_effects=True, vmem_limit_bytes=56 << 20
         ),
         cost_estimate=pl.CostEstimate(flops=3 * 10**10, bytes_accessed=10**8, transcendentals=0),
-    )(own_map[:, :512], row_targets, slots, child_blocks[0], front)
-
-    packed = pl.pallas_call(
-        rows_kernel,
-        out_shape=jax.ShapeDtypeStruct((32 * CAP, 1024), F32),
-        in_specs=[VM, VM],
-        out_specs=VM,
-        name="rows",
-        compiler_params=params(40),
-    )(row_targets, moved)
-    received = lax.all_to_all(
-        packed.reshape(32, CAP, 1024), ("sub", "row"), split_axis=0, concat_axis=0, tiled=True
-    )
-
+    )(col_targets, row_targets, child_map.reshape(2, 16, 512), child_blocks[0], front)
+
+    cols = cols.reshape(2, 1, 2048)
     return pl.pallas_call(
         final_kernel,
         out_shape=jax.ShapeDtypeStruct((512, 2048), F32),
@@ -569,7 +570,7 @@
             SM,
             pl.BlockSpec((2, NB, 16), lambda i: (0, 0, 0)),
             pl.BlockSpec((2, 1, 512), lambda i: (0, 0, i)),
-            pl.BlockSpec((2, 16 * CAP, 1024), lambda i: (0, 0, 0)),
+            pl.BlockSpec((2, 32, CAP, 512), lambda i: (0, 0, 0, 0)),
             pl.BlockSpec((512, 512), lambda i: (0, i)),
             pl.BlockSpec((8, 256, 128), lambda i: (0, 0, 0)),
             pl.BlockSpec((32, 64, 128), lambda i: (0, i, 0)),
@@ -592,7 +593,7 @@
         at,
         slots,
         cols,
-        received.reshape(2, 16 * CAP, 1024),
+        received,
         front,
         own_rows,
         col_rows,

time: 249 us -> 182 us (0.73)
  the two profiles are of different devices: /device:TPU:10 before, /device:TPU:152 now
where the time goes in v3:
time: 182 us; the launch traced here: 181 us
  Pallas kernels  173 us (95%)
  local copies, waits for them, and re-layouts  7.21 us (4%)
    pallas_call x1, Pallas kernels, body(): pl.pallas_call(panel_kernel, out_shape=(jax.ShapeDtypeStruct((PW, PW), F3...  149 us
    pallas_call x1, Pallas kernels, body(): pl.pallas_call(final_kernel, out_shape=jax.ShapeDtypeStruct((512, 2048),...  24.9 us

profile of v3, /device:TPU:152, one launch (start us, length us, event | category | flops | bytes accessed | tf_op | source)
XLA Modules:
  0.0 181.3 jit_solution(1208446586059077662)
XLA Ops:
  0.0 0.6 pad_add_fusion.at_ref
  0.6 1.4 dynamic_slice.12.rmap_ref
  1.9 1.4 dynamic_slice.11.cmap_ref
  3.3 1.5 copy.7
  4.8 148.6 %panel.1 = (f32[512,512]{1,0:T(8,128)}, f32[512,512]{1,0:T(8,128)}, s32[2,32,16]{2,1,0:T(8,128)}, s32[2,64,32]{2,1,0:T(8,128)}, f32[8,256,128]{2,1,0:T(8,128)}, ...) custom-call(s32[1,1024]{1,0:T(1,128)} %dynamic_slice.11.cmap_ref, s32[1,512]{1,0:T(1,128)} %dynamic_slice.12.rmap_ref, ...), custom_call_target="tpu_custom_call" | custom-call | flops 30000001024 | bytes 100000000 | tf_op jit(solution)/shard_map/panel/pallas_call | solution.py:511
  153.4 1.5 reshape.8.col_ref
  154.9 1.5 constant_dynamic-slice_fusion.low_ref
  156.4 24.9 %final.1 = f32[512,2048]{1,0:T(8,128)} custom-call(s32[2]{0:T(128)} %pad_add_fusion.at_ref, s32[2,32,16]{2,1,0:T(8,128)} %get-tuple-element.12.slot_ref, s32[2,1,2048]{2,1,0:T(1,128)} %reshape.8.col_ref, f32[2,32,24,512]{3,2,1,0:T(8,128)} %get-tuple-element.14.x_ref, f32[512,2048]{1,0:T(8,128)} %front_ref.3, f32[8,256,128]{2,1,0:T(8,128)} %get-tuple-element.15.own_ref, ...), custom_call_target="tpu_custom_call" | custom-call | tf_op jit(solution)/shard_map/final/pallas_call | solution.py:565

commit v4 on v3

--- a/solution.py
+++ b/solution.py
@@ -53,33 +53,37 @@
     return (jnp.sum(counts * member, axis=0, keepdims=True) - 1.0).astype(I32)
 
 
-def index_work(rg, cg, map_ref, slot_ref, col_ref):
+def index_work(rg, cg, map_ref, slot_ref, col_ref, flat_ref):
     upto = onehot(iota((512, 512), 0) <= iota((512, 512), 1))
     before64 = onehot(iota((64, 64), 1) < iota((64, 64), 0))
-    before32 = onehot(iota((32, 32), 0) < iota((32, 32), 1))
+    before128 = onehot(iota((128, 128), 0) < iota((128, 128), 1))
     for child in range(2):
-        full = map_ref[child]
-        match = onehot(((full >> 5) & 31) == rg)
+        chunks = [map_ref[child : child + 1, k * 512 : k * 512 + 512] for k in range(16)]
+        match = onehot(((jnp.concatenate(chunks, axis=0) >> 5) & 31) == rg)
         counts = mm(match, upto)
         slots = jnp.zeros((NB, 16), F32)
-        present = jnp.zeros((64, NB), F32)
+        present = jnp.zeros((64, 128), F32)
         for k in range(16):
-            here = full[k : k + 1, :]
+            here = chunks[k]
             block = here >> 5
-            off = jnp.where((here & 31) == iota((NB, 512), 0), F32(1.0), F32(0.0))
+            off = jnp.where((here & 31) == iota((128, 512), 0), F32(1.0), F32(0.0))
             own_rows = onehot(
                 jnp.where((block & 31) == rg, block >> 5, -1) == iota((16, 512), 0)
             )
-            ranked = (off * counts[k : k + 1, :]).astype(BF16)
+            ranked = (off[:NB] * counts[k : k + 1, :]).astype(BF16)
             off = off.astype(BF16)
-            slots = slots + mt(ranked, own_rows) + F32(k * CAP) * mt(off, own_rows)
+            slots = slots + mt(ranked, own_rows) + F32(k * CAP) * mt(off[:NB], own_rows)
             own_cols = onehot(jnp.where((block & 7) == cg, block >> 3, -1) == iota((64, 512), 0))
             present = present + mt(own_cols, off)
         slot_ref[child] = slots.astype(I32) - 1
         pb = present.astype(BF16)
         ahead = jnp.sum(mm(before64, pb), axis=1, keepdims=True)
-        place = ahead + mm(pb, before32)
-        col_ref[child] = jnp.where(present > 0.5, place.astype(I32), -1)
+        place = ahead + mm(pb, before128)
+        flat_ref[...] = jnp.where(present > 0.5, place + 1.0, F32(0.0))
+        flat = flat_ref[pl.ds(0, 16, stride=4), :]
+        for i in range(1, 4):
+            flat = flat + pltpu.roll(flat_ref[pl.ds(i, 16, stride=4), :], NB * i, 1)
+        col_ref[child] = flat.astype(I32) - 1
 
 
 def natural_lower(rg, cg, rows, cols, col0):
@@ -132,11 +136,11 @@
 
 
 def panel_kernel(
-    cmap_ref, rmap_ref, map_ref, child_ref, front_ref,
+    map_ref, child_ref, front_ref,
     low_ref, inv_ref, slot_ref, col_ref, own_ref, cols_ref, got_ref,
     zsend, zrecv, xsend, pan_send, pan_recv, rows_send, rows_recv, piece, swapped, head_send, head_recv, sbuf, w_ref,
     pan_s, pan_r, row_s, row_r, head_s, head_r, own_s, own_r, swap_s, swap_r, piv_s, piv_r,
-    fan_s, fan_r, pass_s, loc_s, z_s, z_r, x_s, x_r,
+    fan_s, fan_r, pass_s, loc_s, z_s, z_r, x_s, x_r, flat_ref, far_s,
 ):
     sub, row, cg = lax.axis_index("sub"), lax.axis_index("row"), lax.axis_index("col")
     rg = sub * 16 + row
@@ -146,6 +150,9 @@
     moves = place != cg
     twin = (1 - sub, row, cg)
 
+    cmap = map_ref[pl.ds(sub, 1), pl.ds(pl.multiple_of(cg * 1024, 1024), 1024)]
+    rmap = map_ref[pl.ds(sub, 1), pl.ds(pl.multiple_of(row * 512, 512), 512)]
+
     def each(first, last, fn):
         def go(q, carry):
             fn(q)
@@ -192,7 +199,7 @@
         for q in range(7, -1, -1):
             n = iota((64, 512), 0)
             nat = ((n >> 5) * 8 + q) * NB + (n & 31)
-            pick = onehot(cmap_ref[:, :512] == nat)
+            pick = onehot(cmap[:, :512] == nat)
             out = mt(pick, high) + mt(pick, low)
             if q == 0:
                 pan_recv[:64, :] = out
@@ -207,7 +214,7 @@
 
     keep = row * 512 + iota((512, 1024), 0) >= cg * 1024 + iota((512, 1024), 1)
     high, low = split(jnp.where(keep, child_ref[...], F32(0.0)))
-    owner = (cmap_ref[...] >> 5) & 7
+    owner = (cmap >> 5) & 7
     slot = owner * 128 + ranks_of(owner, 8, 16)
 
     def bulk_half(h):
@@ -218,13 +225,34 @@
             zsend[h, q] = out[q * 64 : q * 64 + 64, :]
         zrecv[h, cg] = zsend[h, cg]
 
+    last = row // 2
+    for c in range(1, 8):
+
+        @pl.when(c > last)
+        def _(c=c):
+            zrecv[0, c] = jnp.zeros((64, 512), F32)
+            zrecv[1, c] = jnp.zeros((64, 512), F32)
+
+    def bulk_out(h):
+        @pl.when(cg <= last)
+        def _():
+            each(1, 8, lambda q: bulk(h, line(q), cg).start())
+
+    def bulk_in(h):
+        def one(c):
+            @pl.when(c != cg)
+            def _():
+                bulk(h, c, c).wait_recv()
+
+        each(0, last + 1, one)
+
     bulk_half(0)
-    each(1, 8, lambda q: bulk(0, line(q), cg).start())
+    bulk_out(0)
     bulk_half(1)
-    owner = (rmap_ref[...] >> 5) & 31
+    owner = (rmap >> 5) & 31
     slot = owner * CAP + ranks_of(owner, 32, 32)
     pick_rows = onehot(slot == iota((32 * CAP, 512), 0))
-    index_work(rg, cg, map_ref, slot_ref, col_ref)
+    index_work(rg, cg, map_ref, slot_ref, col_ref, flat_ref)
 
     @pl.when(cg != 0)
     def _():
@@ -267,8 +295,24 @@
     def swap():
         return remote(piece, swapped, swap_s, swap_r, mate_id)
 
-    def own(q, at):
-        return remote(piece, own_ref.at[at], own_s.at[q], own_r.at[at], (sub, row, line(q)))
+    def own_up(t, at, src):
+        return remote(src, own_ref.at[at], own_s.at[t], own_r.at[at], (sub, row, line(1)))
+
+    def own_down(t, at, src):
+        return remote(src, own_ref.at[at], own_s.at[4 + t], own_r.at[at], (sub, row, line(7)))
+
+    def ring(t):
+        @pl.when(t < 4)
+        def _():
+            at = (cg + 8 - t) % 8
+            own_up(t, at, own_ref.at[at]).wait_recv()
+            own_up(t, at, own_ref.at[at]).start()
+
+        @pl.when(t < 3)
+        def _():
+            at = (cg + t) % 8
+            own_down(t, at, own_ref.at[at]).wait_recv()
+            own_down(t, at, own_ref.at[at]).start()
 
     own_local = pltpu.make_async_copy(piece, own_ref.at[cg], loc_s.at[0])
 
@@ -281,22 +325,47 @@
         swap().start()
 
     head_recv[cg] = head_send[...]
-    each(1, 8, lambda q: bulk(1, line(q), cg).start())
-
-    def cross(h, q, at):
-        p, device = plane(q)
-        return remote(xsend.at[h, p], got_ref.at[h, at], x_s.at[h, p], x_r.at[h, at], device)
+    bulk_out(1)
+
+    def cross(h, p, at, level):
+        lanes = pl.ds(0, 128 * (level + 1))
+        return remote(
+            xsend.at[h, p, :, lanes], got_ref.at[h, at, :, lanes], x_s.at[h, p], x_r.at[h, at],
+            (p // 16, p % 16, cg),
+        )
+
+    def by_level(fn):
+        for level in range(4):
+
+            @pl.when(row // 4 == level)
+            def _(level=level):
+                each(1, 32, lambda q: fn(plane(q)[0], level))
+
+    def cross_out(h):
+        by_level(lambda p, level: cross(h, p, rg, level).start())
+
+    def cross_in(h):
+        for level in range(4):
+
+            def one(j):
+                p = j // 4 * 16 + level * 4 + j % 4
+
+                @pl.when(p != rg)
+                def _():
+                    cross(h, p, p, level).wait_recv()
+
+            each(0, 8, one)
 
     def keep_own(h):
         return pltpu.make_async_copy(xsend.at[h, rg], got_ref.at[h, rg], loc_s.at[2 + h])
 
     def cross_half(h):
-        each(1, 8, lambda q: bulk(h, line(q), line(q)).wait_recv())
+        bulk_in(h)
         high, low = split(zrecv[h].reshape(512, 512))
         out = mt(pick_rows, high) + mt(pick_rows, low)
         for p in range(32):
             xsend[h, p] = out[p * CAP : p * CAP + CAP, :]
-        each(1, 32, lambda q: cross(h, q, rg).start())
+        cross_out(h)
         keep_own(h).start()
 
     def pivot(q, at):
@@ -325,20 +394,50 @@
     def _():
         swapped[...] = piece[...]
 
-    def fan(q, at):
-        return remote(swapped, cols_ref.at[at], fan_s.at[q], fan_r.at[at], chip(q)[1])
+    gx, gy = row // 4, row % 4
+
+    def xmate(j):
+        return (gx + j) % 4 * 4 + gy
+
+    def ymate(j):
+        return gx * 4 + (gy + j) % 4
+
+    def fan(k, at, to):
+        return remote(swapped, cols_ref.at[at], fan_s.at[k], fan_r.at[0, at], (sub, to, cg))
+
+    def far(half, k, at, to):
+        part = cols_ref.at[at, pl.ds(half * 128, 128)]
+        return remote(part, part, far_s.at[half, k], fan_r.at[half, at], (sub, to, cg))
 
     def hand(at, src):
-        return remote(src, cols_ref.at[at], pass_s.at[at % 16], fan_r.at[at], twin)
-
-    def twin_hand(at):
-        return remote(swapped, cols_ref.at[at], pass_s.at[at % 16], fan_r.at[at], twin)
+        return remote(src, cols_ref.at[at], pass_s.at[at % 16], fan_r.at[0, at], twin)
+
+    def near(j):
+        x, y = xmate(j), ymate(j)
+        fan(j, sub * 16 + x, x).wait_recv()
+        each(1, 4, lambda i: far(0, j * 4 + i, sub * 16 + x, ymate(i)).start())
+        hand(sub * 16 + x, cols_ref.at[sub * 16 + x]).start()
+        fan(4 + j, sub * 16 + y, y).wait_recv()
+        each(1, 4, lambda i: far(1, j * 4 + i, sub * 16 + y, xmate(i)).start())
+        hand(sub * 16 + y, cols_ref.at[sub * 16 + y]).start()
+
+    def corner(i, j):
+        at = sub * 16 + (gx + i) % 4 * 4 + (gy + j) % 4
+        far(0, 0, at, 0).wait_recv()
+        far(1, 0, at, 0).wait_recv()
+        hand(at, cols_ref.at[at]).start()
 
     cols_local = pltpu.make_async_copy(swapped, cols_ref.at[rg], loc_s.at[1])
-    each(1, 16, lambda q: fan(q, rg).start())
+
+    def fan_out(j):
+        fan(j, rg, xmate(j)).start()
+        fan(4 + j, rg, ymate(j)).start()
+
+    each(1, 4, fan_out)
     hand(rg, swapped).start()
     cols_local.start()
-    each(1, 8, lambda q: own(q, cg).start())
+    own_up(0, cg, piece).start()
+    own_down(0, cg, piece).start()
     own_local.start()
 
     @pl.when(sub == 0)
@@ -374,14 +473,15 @@
         w_ref[pl.ds(at, 128), :] = jnp.concatenate([ahead, rows[:, PW:]], axis=1)
         w_ref[pl.ds(at, 128), pl.ds(at, 128)] = upper
 
-        def relay(q):
-            @pl.when(q < 16)
-            def _():
-                r = chip(q)[0]
-                fan(q, sub * 16 + r).wait_recv()
-                hand(sub * 16 + r, cols_ref.at[sub * 16 + r]).start()
-
-        each(kb * 4 + 1, kb * 4 + 5, relay)
+        ring(kb + 1)
+
+        @pl.when(kb == 0)
+        def _():
+            each(1, 4, near)
+
+        @pl.when(kb > 0)
+        def _():
+            each(1, 4, lambda j: corner(kb, j))
 
         @pl.when(kb < 2)
         def _():
@@ -390,25 +490,39 @@
         return carry
 
     lax.fori_loop(0, PW // 128, step, 0)
-    low_ref[...] = w_ref[:, :PW].T
+    w_ref[:, :PW] = w_ref[:, :PW].T
+    low_ref[...] = w_ref[pl.ds(pl.multiple_of(jnp.minimum(rg, 15) * NB, NB), NB), :PW]
     turned = w_ref[:, PW:].T
     for c8 in range(8):
         for half in range(2):
             src = (half * 8 + c8) * NB
             inv_ref[(c8 * 2 + half) * NB : (c8 * 2 + half + 1) * NB, :] = turned[src : src + NB, :]
 
-    each(0, 16, lambda q: twin_hand((1 - sub) * 16 + q).wait_recv())
-    each(0, 16, lambda q: twin_hand(sub * 16 + q).wait_send())
-    each(1, 16, lambda q: fan(q, rg).wait_send())
-    each(1, 8, lambda q: own(q, line(q)).wait_recv())
-    each(1, 8, lambda q: own(q, cg).wait_send())
+    each(0, 16, lambda q: hand((1 - sub) * 16 + q, swapped).wait_recv())
+    each(0, 16, lambda q: hand(sub * 16 + q, swapped).wait_send())
+
+    def sent(j):
+        fan(j, rg, xmate(j)).wait_send()
+        fan(4 + j, rg, ymate(j)).wait_send()
+        each(1, 4, lambda i: far(0, j * 4 + i, rg, ymate(i)).wait_send())
+        each(1, 4, lambda i: far(1, j * 4 + i, rg, xmate(i)).wait_send())
+
+    each(1, 4, sent)
+    own_up(0, line(4), piece).wait_recv()
+    own_down(0, line(3), piece).wait_recv()
+    each(0, 4, lambda t: own_up(t, cg, piece).wait_send())
+    each(0, 3, lambda t: own_down(t, cg, piece).wait_send())
     own_local.wait()
     cols_local.wait()
     each(1, 32, lambda q: to_plane(q).wait_send())
     for h in range(2):
-        each(1, 8, lambda q: bulk(h, line(q), cg).wait_send())
-        each(1, 32, lambda q: cross(h, q, plane(q)[0]).wait_recv())
-        each(1, 32, lambda q: cross(h, q, rg).wait_send())
+
+        @pl.when(cg <= last)
+        def _(h=h):
+            each(1, 8, lambda q: bulk(h, line(q), cg).wait_send())
+
+        cross_in(h)
+        by_level(lambda p, level: cross(h, p, rg, level).wait_send())
         keep_own(h).wait()
 
     @pl.when(cg == 0)
@@ -469,6 +583,9 @@
             pick = row_picker(slot_ref[child], 16 * CAP)
             for h in range(2):
                 got = x_ref[h, child * 16 : child * 16 + 16].reshape(16 * CAP, 512)
+                r, lane = iota(got.shape, 0), iota(got.shape, 1)
+                limit = jnp.where(r < 4 * CAP, 128, jnp.where(r < 8 * CAP, 256, 384))
+                got = jnp.where((lane < limit) | (r >= 12 * CAP), got, F32(0.0))
                 high, low = split(got)
                 at = pl.ds(h * 512, 512)
                 yh[child, :, at], yl[child, :, at] = split(mm(pick, high) + mm(pick, low))
@@ -478,60 +595,66 @@
     for i in range(4):
         tile = unpack([cols_ref[i * 8 + c] for c in range(8)], left)
         parts.append(three(split(tile), inv, mm))
-    cols = jnp.concatenate(
-        [parts[i][q * NB : q * NB + NB] for q in range(4) for i in range(4)], axis=0
+    cols = split(
+        jnp.concatenate(
+            [parts[i][q * NB : q * NB + NB] for q in range(4) for i in range(4)], axis=0
+        )
     )
-    total = front_ref[...] - three((fh[...], fl[...]), split(cols), mt)
-    for child in range(2):
-        m = col_ref[child]
-        m = jnp.where(m < 0, -1, ((m >> 6) & 1) * 512 + (m >> 7) * 64 + (m & 63))
-        put = onehot(m == iota((1024, 512), 0))
-        total = total + mm(yh[child], put) + mm(yl[child], put)
-    total = jnp.where(natural_lower(rg, cg, 512, 512, ct * 512), total, F32(0.0))
-    o_ref[...] = total
-
-    @pl.when(ct == 0)
-    def _():
-        lane = iota((512, 128), 1)
-        value = jnp.where(
-            natural_lower(rg, cg, 512, 128, 0), panel_ref[...], F32(0.0)
-        )
-        o_ref[:, :128] = jnp.where(lane < 64, value, total[:, :128])
+    for v in range(4):
+
+        @pl.when(ct == v)
+        def _(v=v):
+            top = v * 128
+            down = pl.ds(top, 512 - top)
+            total = front_ref[down, :] - three((fh[down, :], fl[down, :]), cols, mt)
+            for child in range(2):
+                m = jnp.concatenate(
+                    [col_ref[child, v * 4 + j : v * 4 + j + 1, :] for j in range(4)], axis=1
+                )
+                m = jnp.where(m < 0, -1, ((m >> 6) & 1) * 512 + (m >> 7) * 64 + (m & 63))
+                put = onehot(m == iota((1024, 512), 0))
+                total = total + mm(yh[child, down, :], put) + mm(yl[child, down, :], put)
+            r, c = top + iota(total.shape, 0), v * 512 + iota(total.shape, 1)
+            nat_row = ((r >> 5) * 32 + rg) * 32 + (r & 31)
+            nat_col = ((c >> 5) * 8 + cg) * 32 + (c & 31)
+            total = jnp.where(nat_row >= nat_col, total, F32(0.0))
+            if v == 0:
+                lane = iota((512, 128), 1)
+                value = jnp.where(natural_lower(rg, cg, 512, 128, 0), panel_ref[...], F32(0.0))
+                o_ref[:, :128] = jnp.where(lane < 64, value, total[:, :128])
+                o_ref[:, 128:] = total[:, 128:]
+            else:
+                o_ref[:top, :] = jnp.zeros((top, 512), F32)
+                o_ref[down, :] = total
 
 
 def body(front, child_blocks, child_map):
     sub, row, cg = lax.axis_index("sub"), lax.axis_index("row"), lax.axis_index("col")
     rg = sub * 16 + row
     at = jnp.stack([rg, cg]).astype(I32)
-    own_map = lax.dynamic_index_in_dim(child_map, sub, 0, keepdims=True)
-    row_targets = lax.dynamic_slice_in_dim(own_map, row * 512, 512, axis=1)
-    col_targets = lax.dynamic_slice_in_dim(own_map, cg * 1024, 1024, axis=1)
-
     DMA = pltpu.SemaphoreType.DMA
     lower, inverse, slots, cols, own_rows, col_rows, received = pl.pallas_call(
         panel_kernel,
         out_shape=(
-            jax.ShapeDtypeStruct((PW, PW), F32),
+            jax.ShapeDtypeStruct((NB, PW), F32),
             jax.ShapeDtypeStruct((PW, PW), F32),
             jax.ShapeDtypeStruct((2, NB, 16), I32),
-            jax.ShapeDtypeStruct((2, 64, NB), I32),
+            jax.ShapeDtypeStruct((2, 16, 128), I32),
             jax.ShapeDtypeStruct((8, 256, 128), F32),
             jax.ShapeDtypeStruct((32, 256, 128), F32),
             jax.ShapeDtypeStruct((2, 32, CAP, 512), F32),
         ),
         grid=(1,),
         in_specs=[
-            pl.BlockSpec((1, 1024), lambda i: (0, 0)),
-            pl.BlockSpec((1, 512), lambda i: (0, 0)),
-            pl.BlockSpec((2, 16, 512), lambda i: (0, 0, 0)),
+            pl.BlockSpec((2, 8192), lambda i: (0, 0)),
             pl.BlockSpec((512, 1024), lambda i: (0, 0)),
             pl.BlockSpec((512, 128), lambda i: (0, 0)),
         ],
         out_specs=(
-            pl.BlockSpec((PW, PW), lambda i: (0, 0)),
+            pl.BlockSpec((NB, PW), lambda i: (0, 0)),
             pl.BlockSpec((PW, PW), lambda i: (0, 0)),
             pl.BlockSpec((2, NB, 16), lambda i: (0, 0, 0)),
-            pl.BlockSpec((2, 64, NB), lambda i: (0, 0, 0)),
+            pl.BlockSpec((2, 16, 128), lambda i: (0, 0, 0)),
             pl.BlockSpec(memory_space=pl.ANY),
             pl.BlockSpec(memory_space=pl.ANY),
             pl.BlockSpec(memory_space=pl.ANY),
@@ -551,17 +674,17 @@
             pltpu.VMEM((16, NB, PW), F32),
             pltpu.VMEM((PW, 2 * PW), F32),
             DMA((8,)), DMA, DMA((32,)), DMA((32,)), DMA((8,)), DMA((8,)), DMA((8,)), DMA((8,)),
-            DMA, DMA, DMA((32,)), DMA((16,)), DMA((16,)), DMA((32,)), DMA((16,)), DMA((4,)),
+            DMA, DMA, DMA((32,)), DMA((16,)), DMA((8,)), DMA((2, 32)), DMA((16,)), DMA((4,)),
             DMA((2, 8)), DMA((2, 8)), DMA((2, 32)), DMA((2, 32)),
+            pltpu.VMEM((64, 128), F32), DMA((2, 16)),
         ],
         name="panel",
         compiler_params=pltpu.CompilerParams(
             collective_id=1, has_side_effects=True, vmem_limit_bytes=56 << 20
         ),
         cost_estimate=pl.CostEstimate(flops=3 * 10**10, bytes_accessed=10**8, transcendentals=0),
-    )(col_targets, row_targets, child_map.reshape(2, 16, 512), child_blocks[0], front)
-
-    cols = cols.reshape(2, 1, 2048)
+    )(child_map, child_blocks[0], front)
+
     return pl.pallas_call(
         final_kernel,
         out_shape=jax.ShapeDtypeStruct((512, 2048), F32),
@@ -569,7 +692,7 @@
         in_specs=[
             SM,
             pl.BlockSpec((2, NB, 16), lambda i: (0, 0, 0)),
-            pl.BlockSpec((2, 1, 512), lambda i: (0, 0, i)),
+            pl.BlockSpec((2, 16, 128), lambda i: (0, 0, 0)),
             pl.BlockSpec((2, 32, CAP, 512), lambda i: (0, 0, 0, 0)),
             pl.BlockSpec((512, 512), lambda i: (0, i)),
             pl.BlockSpec((8, 256, 128), lambda i: (0, 0, 0)),
@@ -598,7 +721,7 @@
         own_rows,
         col_rows,
         inverse,
-        lax.dynamic_slice_in_dim(lower, jnp.minimum(rg, 15) * NB, NB, axis=0),
+        lower,
     )
 
 

time: 182 us -> 165 us (0.907)
  the two profiles are of different devices: /device:TPU:152 before, /device:TPU:232 now
where the time goes in v4:
time: 165 us
  Pallas kernels  164 us (99%)
    pallas_call x1, Pallas kernels, body(): pl.pallas_call(panel_kernel, out_shape=(jax.ShapeDtypeStruct((NB, PW), F3...  143 us
    pallas_call x1, Pallas kernels, body(): pl.pallas_call(final_kernel, out_shape=jax.ShapeDtypeStruct((512, 2048),...  21.8 us

profile of v4, /device:TPU:232, one launch (start us, length us, event | category | flops | bytes accessed | tf_op | source)
XLA Modules:
  0.0 165.1 jit_solution(5674228830825139213)
XLA Ops:
  0.0 0.7 pad_add_fusion.at_ref
  0.7 142.7 %panel.1 = (f32[32,512]{1,0:T(8,128)}, f32[512,512]{1,0:T(8,128)}, s32[2,32,16]{2,1,0:T(8,128)}, s32[2,16,128]{2,1,0:T(8,128)}, f32[8,256,128]{2,1,0:T(8,128)}, ...) custom-call(s32[2,8192]{1,0:T(2,128)} %map_ref.1, f32[512,1024]{1,0:T(8,128)} %bitcast.3, f32[512,2048]{1,0:T(8,128)} %front_ref.3), custom_call_target="tpu_custom_call" | custom-call | flops 30000001024 | bytes 100000000 | tf_op jit(solution)/shard_map/panel/pallas_call | solution.py:636
  143.3 21.8 %final.1 = f32[512,2048]{1,0:T(8,128)} custom-call(s32[2]{0:T(128)} %pad_add_fusion.at_ref, s32[2,32,16]{2,1,0:T(8,128)} %get-tuple-element.12.slot_ref, s32[2,16,128]{2,1,0:T(8,128)} %get-tuple-element.13.col_ref, f32[2,32,24,512]{3,2,1,0:T(8,128)} %get-tuple-element.14.x_ref, f32[512,2048]{1,0:T(8,128)} %front_ref.3, ...), custom_call_target="tpu_custom_call" | custom-call | tf_op jit(solution)/shard_map/final/pallas_call | solution.py:688

commit v5 on v4

--- a/solution.py
+++ b/solution.py
@@ -98,22 +98,35 @@
     return jnp.concatenate(parts, axis=0)
 
 
+GROUP = 8
+
+
 def sweep(w):
-    tiles = [w[8 * i : 8 * i + 8, :] for i in range(16)]
-    lane = iota((8, 128), 1)
-    sub = iota((8, 128), 0)
-    for k in range(128):
-        own, s = k // 8, k % 8
-        row = tiles[own][s : s + 1, :]
-        inv = 1.0 / row[:, k : k + 1]
-        pivot_row = jnp.where(lane[:1] == k, F32(1.0), row)
-        scaled = pivot_row * inv
-        for i in range(own, 16):
-            t = tiles[i]
-            col = t[:, k : k + 1]
-            new = jnp.where(lane == k, F32(0.0), t) - col * scaled
-            tiles[i] = jnp.where(sub > s, new, t) if i == own else new
-    w = jnp.concatenate(tiles, axis=0)
+    lane = iota((1, 128), 1)
+    below = w
+    done = []
+    for k0 in range(0, 128, GROUP):
+        n = 128 - k0
+        column = [jnp.broadcast_to(below[:, k0 + j : k0 + j + 1], (n, 128)) for j in range(GROUP)]
+        row = [below[j : j + 1, :] for j in range(GROUP)]
+        scaled = []
+        for j in range(GROUP):
+            inv = 1.0 / column[j][j : j + 1, :]
+            scaled.append(jnp.where(lane == k0 + j, F32(1.0), row[j]) * inv)
+            for i in range(j + 1, GROUP):
+                ratio = column[i][j : j + 1, :] * inv
+                kept = jnp.where(lane == k0 + j, F32(0.0), row[i])
+                row[i] = kept - column[j][i : i + 1, :] * scaled[j]
+                column[i] = column[i] - column[j] * ratio
+        done.extend(row)
+        if n > GROUP:
+            inside = (lane >= k0) & (lane < k0 + GROUP)
+            rest = jnp.where(inside, F32(0.0), below[GROUP:])
+            for j in range(GROUP):
+                part = jnp.where((lane > k0 + j) & inside, F32(0.0), scaled[j])
+                rest = rest - column[j][GROUP:] * part
+            below = rest
+    w = jnp.concatenate(done, axis=0)
     r, c = iota((128, 128), 0), iota((128, 128), 1)
     diag = jnp.sum(jnp.where(r == c, w, F32(0.0)), axis=1, keepdims=True)
     scale = 1.0 / jnp.sqrt(diag)
@@ -196,16 +209,14 @@
     def _():
         keep = row * 512 + iota((512, 512), 0) >= iota((512, 512), 1)
         high, low = split(jnp.where(keep, child_ref[:, :512], F32(0.0)))
-        for q in range(7, -1, -1):
-            n = iota((64, 512), 0)
-            nat = ((n >> 5) * 8 + q) * NB + (n & 31)
-            pick = onehot(cmap[:, :512] == nat)
-            out = mt(pick, high) + mt(pick, low)
-            if q == 0:
-                pan_recv[:64, :] = out
-            else:
-                pan_send[q] = out
-                to_line(q).start()
+        n = iota((512, 512), 0)
+        nat = (((n >> 5) & 1) * 8 + (n >> 6)) * NB + (n & 31)
+        pick = onehot(cmap[:, :512] == nat)
+        out = mt(pick, high) + mt(pick, low)
+        for q in range(1, 8):
+            pan_send[q] = out[q * 64 : q * 64 + 64, :]
+            to_line(q).start()
+        pan_recv[:64, :] = out[:64, :]
 
     def bulk(h, q, at):
         return remote(
@@ -247,7 +258,6 @@
         each(0, last + 1, one)
 
     bulk_half(0)
-    bulk_out(0)
     bulk_half(1)
     owner = (rmap >> 5) & 31
     slot = owner * CAP + ranks_of(owner, 32, 32)
@@ -257,6 +267,8 @@
     @pl.when(cg != 0)
     def _():
         to_line(cg).wait_recv()
+
+    bulk_out(0)
 
     high, low = split(pan_recv[...])
     out = mt(pick_rows, high) + mt(pick_rows, low)
@@ -325,7 +337,6 @@
         swap().start()
 
     head_recv[cg] = head_send[...]
-    bulk_out(1)
 
     def cross(h, p, at, level):
         lanes = pl.ds(0, 128 * (level + 1))
@@ -386,6 +397,8 @@
         each(1, 16, lambda q: pivot(q, row).start())
         pivot_twin(row).start()
 
+    bulk_out(1)
+
     @pl.when(moves)
     def _():
         swap().wait_recv()
@@ -439,6 +452,8 @@
     own_up(0, cg, piece).start()
     own_down(0, cg, piece).start()
     own_local.start()
+
+    cross_half(0)
 
     @pl.when(sub == 0)
     def _():
@@ -483,9 +498,9 @@
         def _():
             each(1, 4, lambda j: corner(kb, j))
 
-        @pl.when(kb < 2)
+        @pl.when(kb == 1)
         def _():
-            cross_half(kb)
+            cross_half(1)
 
         return carry
 

time: 165 us -> 139 us (0.84)
  the two profiles are of different devices: /device:TPU:232 before, /device:TPU:132 now
where the time goes in v5:
time: 139 us
  Pallas kernels  138 us (99%)
    pallas_call x1, Pallas kernels, body(): pl.pallas_call(panel_kernel, out_shape=(jax.ShapeDtypeStruct((NB, PW), F3...  116 us
    pallas_call x1, Pallas kernels, body(): pl.pallas_call(final_kernel, out_shape=jax.ShapeDtypeStruct((512, 2048),...  21.8 us

profile of v5, /device:TPU:132, one launch (start us, length us, event | category | flops | bytes accessed | tf_op | source)
XLA Modules:
  0.0 138.6 jit_solution(2485269267083340200)
XLA Ops:
  0.0 0.7 pad_add_fusion.at_ref
  0.7 116.1 %panel.1 = (f32[32,512]{1,0:T(8,128)}, f32[512,512]{1,0:T(8,128)}, s32[2,32,16]{2,1,0:T(8,128)}, s32[2,16,128]{2,1,0:T(8,128)}, f32[8,256,128]{2,1,0:T(8,128)}, ...) custom-call(s32[2,8192]{1,0:T(2,128)} %map_ref.1, f32[512,1024]{1,0:T(8,128)} %bitcast.3, f32[512,2048]{1,0:T(8,128)} %front_ref.3), custom_call_target="tpu_custom_call" | custom-call | flops 30000001024 | bytes 100000000 | tf_op jit(solution)/shard_map/panel/pallas_call | solution.py:651
  116.8 21.8 %final.1 = f32[512,2048]{1,0:T(8,128)} custom-call(s32[2]{0:T(128)} %pad_add_fusion.at_ref, s32[2,32,16]{2,1,0:T(8,128)} %get-tuple-element.12.slot_ref, s32[2,16,128]{2,1,0:T(8,128)} %get-tuple-element.13.col_ref, f32[2,32,24,512]{3,2,1,0:T(8,128)} %get-tuple-element.14.x_ref, f32[512,2048]{1,0:T(8,128)} %front_ref.3, ...), custom_call_target="tpu_custom_call" | custom-call | tf_op jit(solution)/shard_map/final/pallas_call | solution.py:703

commit v6 on v5

--- a/solution.py
+++ b/solution.py
@@ -141,6 +141,21 @@
     )
 
 
+def unpack(pieces, left):
+    top, bottom = [], []
+    for p in range(4):
+        a, b = pieces[2 * p], pieces[2 * p + 1]
+        top.append(jnp.where(left, a, pltpu.roll(b, 64, 1)))
+        bottom.append(jnp.where(left, pltpu.roll(a, 64, 1), b))
+    return jnp.concatenate(
+        [jnp.concatenate(top, axis=1), jnp.concatenate(bottom, axis=1)], axis=0
+    )
+
+
+def three(a, b, dot):
+    return dot(a[0], b[0]) + (dot(a[0], b[1]) + dot(a[1], b[0]))
+
+
 def remote(src, dst, send, recv, device):
     return pltpu.make_async_remote_copy(
         src_ref=src, dst_ref=dst, send_sem=send, recv_sem=recv, device_id=device,
@@ -150,7 +165,8 @@
 
 def panel_kernel(
     map_ref, child_ref, front_ref,
-    low_ref, inv_ref, slot_ref, col_ref, own_ref, cols_ref, got_ref,
+    slot_ref, col_ref, acc_ref, panel_ref, got_ref,
+    own_ref, cols_ref, inv_ref, ih, il, fh, fl,
     zsend, zrecv, xsend, pan_send, pan_recv, rows_send, rows_recv, piece, swapped, head_send, head_recv, sbuf, w_ref,
     pan_s, pan_r, row_s, row_r, head_s, head_r, own_s, own_r, swap_s, swap_r, piv_s, piv_r,
     fan_s, fan_r, pass_s, loc_s, z_s, z_r, x_s, x_r, flat_ref, far_s,
@@ -505,15 +521,49 @@
         return carry
 
     lax.fori_loop(0, PW // 128, step, 0)
-    w_ref[:, :PW] = w_ref[:, :PW].T
-    low_ref[...] = w_ref[pl.ds(pl.multiple_of(jnp.minimum(rg, 15) * NB, NB), NB), :PW]
     turned = w_ref[:, PW:].T
     for c8 in range(8):
         for half in range(2):
             src = (half * 8 + c8) * NB
             inv_ref[(c8 * 2 + half) * NB : (c8 * 2 + half + 1) * NB, :] = turned[src : src + NB, :]
+    ih[...], il[...] = split(inv_ref[...])
+    w_ref[:, :PW] = w_ref[:, :PW].T
+    known = w_ref[pl.ds(pl.multiple_of(jnp.minimum(rg, 15) * NB, NB), NB), :PW]
+
+    own_up(0, line(4), piece).wait_recv()
+    own_down(0, line(3), piece).wait_recv()
+    own_local.wait()
+    for t in range(4):
+        tile = unpack([own_ref[c, t * 64 : t * 64 + 64, :] for c in range(8)], left)
+        rows = three(split(tile), (ih[...], il[...]), mm)
+        if t == 0:
+            keep = (iota((128, PW), 0) < NB) & (rg < 16)
+            rows = jnp.where(
+                keep, jnp.concatenate([known, jnp.zeros((128 - NB, PW), F32)], axis=0), rows
+            )
+        fh[t * 128 : t * 128 + 128, :], fl[t * 128 : t * 128 + 128, :] = split(rows)
+    lane = iota((PW, 128), 1)
+    nat = ((lane >> 5) * 8 + cg) * 32 + (lane & 31)
+    pick = onehot((nat == iota((PW, 128), 0)) & (lane < 64))
+    panel_ref[...] = mm(fh[...], pick) + mm(fl[...], pick)
 
     each(0, 16, lambda q: hand((1 - sub) * 16 + q, swapped).wait_recv())
+    cols_local.wait()
+    for v in range(4):
+        parts = []
+        for i in range(4):
+            tile = unpack(
+                [cols_ref[i * 8 + c, v * 64 : v * 64 + 64, :] for c in range(8)], left
+            )
+            parts.append(three(split(tile), (ih[...], il[...]), mm))
+        cols = split(
+            jnp.concatenate(
+                [parts[i][q * NB : q * NB + NB] for q in range(4) for i in range(4)], axis=0
+            )
+        )
+        down = pl.ds(v * 128, 512 - v * 128)
+        acc_ref[down, pl.ds(v * 512, 512)] = three((fh[down, :], fl[down, :]), cols, mt)
+
     each(0, 16, lambda q: hand(sub * 16 + q, swapped).wait_send())
 
     def sent(j):
@@ -523,12 +573,8 @@
         each(1, 4, lambda i: far(1, j * 4 + i, rg, xmate(i)).wait_send())
 
     each(1, 4, sent)
-    own_up(0, line(4), piece).wait_recv()
-    own_down(0, line(3), piece).wait_recv()
     each(0, 4, lambda t: own_up(t, cg, piece).wait_send())
     each(0, 3, lambda t: own_down(t, cg, piece).wait_send())
-    own_local.wait()
-    cols_local.wait()
     each(1, 32, lambda q: to_plane(q).wait_send())
     for h in range(2):
 
@@ -555,45 +601,14 @@
         each(0, 16, lambda q: pivot_twin(q).wait_send())
 
 
-def unpack(pieces, left):
-    top, bottom = [], []
-    for p in range(4):
-        a, b = pieces[2 * p], pieces[2 * p + 1]
-        top.append(jnp.where(left, a, pltpu.roll(b, 64, 1)))
-        bottom.append(jnp.where(left, pltpu.roll(a, 64, 1), b))
-    return jnp.concatenate(
-        [jnp.concatenate(top, axis=1), jnp.concatenate(bottom, axis=1)], axis=0
-    )
-
-
-def three(a, b, dot):
-    return dot(a[0], b[0]) + (dot(a[0], b[1]) + dot(a[1], b[0]))
-
-
 def final_kernel(
-    at_ref, slot_ref, col_ref, x_ref, front_ref, own_ref, cols_ref, inv_ref, low_ref,
-    o_ref, ih, il, fh, fl, yh, yl, panel_ref,
+    at_ref, slot_ref, col_ref, x_ref, front_ref, acc_ref, panel_ref, o_ref, yh, yl,
 ):
     rg, cg = at_ref[0], at_ref[1]
     ct = pl.program_id(0)
-    left = iota((64, 128), 1) < 64
 
     @pl.when(ct == 0)
     def _():
-        ih[...], il[...] = split(inv_ref[...])
-        inv = ih[...], il[...]
-        for t in range(4):
-            tile = unpack([own_ref[c, t * 64 : t * 64 + 64, :] for c in range(8)], left)
-            rows = three(split(tile), inv, mm)
-            if t == 0:
-                keep = (iota((128, PW), 0) < NB) & (rg < 16)
-                known = jnp.concatenate([low_ref[...], jnp.zeros((128 - NB, PW), F32)], axis=0)
-                rows = jnp.where(keep, known, rows)
-            fh[t * 128 : t * 128 + 128, :], fl[t * 128 : t * 128 + 128, :] = split(rows)
-        lane = iota((PW, 128), 1)
-        nat = ((lane >> 5) * 8 + cg) * 32 + (lane & 31)
-        pick = onehot((nat == iota((PW, 128), 0)) & (lane < 64))
-        panel_ref[...] = mm(fh[...], pick) + mm(fl[...], pick)
         for child in range(2):
             pick = row_picker(slot_ref[child], 16 * CAP)
             for h in range(2):
@@ -605,23 +620,13 @@
                 at = pl.ds(h * 512, 512)
                 yh[child, :, at], yl[child, :, at] = split(mm(pick, high) + mm(pick, low))
 
-    inv = ih[...], il[...]
-    parts = []
-    for i in range(4):
-        tile = unpack([cols_ref[i * 8 + c] for c in range(8)], left)
-        parts.append(three(split(tile), inv, mm))
-    cols = split(
-        jnp.concatenate(
-            [parts[i][q * NB : q * NB + NB] for q in range(4) for i in range(4)], axis=0
-        )
-    )
     for v in range(4):
 
         @pl.when(ct == v)
         def _(v=v):
             top = v * 128
             down = pl.ds(top, 512 - top)
-            total = front_ref[down, :] - three((fh[down, :], fl[down, :]), cols, mt)
+            total = front_ref[down, :] - acc_ref[down, :]
             for child in range(2):
                 m = jnp.concatenate(
                     [col_ref[child, v * 4 + j : v * 4 + j + 1, :] for j in range(4)], axis=1
@@ -648,15 +653,13 @@
     rg = sub * 16 + row
     at = jnp.stack([rg, cg]).astype(I32)
     DMA = pltpu.SemaphoreType.DMA
-    lower, inverse, slots, cols, own_rows, col_rows, received = pl.pallas_call(
+    slots, cols, product, panel, received = pl.pallas_call(
         panel_kernel,
         out_shape=(
-            jax.ShapeDtypeStruct((NB, PW), F32),
-            jax.ShapeDtypeStruct((PW, PW), F32),
             jax.ShapeDtypeStruct((2, NB, 16), I32),
             jax.ShapeDtypeStruct((2, 16, 128), I32),
-            jax.ShapeDtypeStruct((8, 256, 128), F32),
-            jax.ShapeDtypeStruct((32, 256, 128), F32),
+            jax.ShapeDtypeStruct((512, 2048), F32),
+            jax.ShapeDtypeStruct((512, 128), F32),
             jax.ShapeDtypeStruct((2, 32, CAP, 512), F32),
         ),
         grid=(1,),
@@ -666,15 +669,20 @@
             pl.BlockSpec((512, 128), lambda i: (0, 0)),
         ],
         out_specs=(
-            pl.BlockSpec((NB, PW), lambda i: (0, 0)),
-            pl.BlockSpec((PW, PW), lambda i: (0, 0)),
             pl.BlockSpec((2, NB, 16), lambda i: (0, 0, 0)),
             pl.BlockSpec((2, 16, 128), lambda i: (0, 0, 0)),
-            pl.BlockSpec(memory_space=pl.ANY),
-            pl.BlockSpec(memory_space=pl.ANY),
+            pl.BlockSpec((512, 2048), lambda i: (0, 0)),
+            pl.BlockSpec((512, 128), lambda i: (0, 0)),
             pl.BlockSpec(memory_space=pl.ANY),
         ),
         scratch_shapes=[
+            pltpu.VMEM((8, 256, 128), F32),
+            pltpu.VMEM((32, 256, 128), F32),
+            pltpu.VMEM((PW, PW), F32),
+            pltpu.VMEM((PW, PW), BF16),
+            pltpu.VMEM((PW, PW), BF16),
+            pltpu.VMEM((512, PW), BF16),
+            pltpu.VMEM((512, PW), BF16),
             pltpu.VMEM((2, 8, 64, 512), F32),
             pltpu.VMEM((2, 8, 64, 512), F32),
             pltpu.VMEM((2, 32, CAP, 512), F32),
@@ -710,20 +718,13 @@
             pl.BlockSpec((2, 16, 128), lambda i: (0, 0, 0)),
             pl.BlockSpec((2, 32, CAP, 512), lambda i: (0, 0, 0, 0)),
             pl.BlockSpec((512, 512), lambda i: (0, i)),
-            pl.BlockSpec((8, 256, 128), lambda i: (0, 0, 0)),
-            pl.BlockSpec((32, 64, 128), lambda i: (0, i, 0)),
-            pl.BlockSpec((PW, PW), lambda i: (0, 0)),
-            pl.BlockSpec((NB, PW), lambda i: (0, 0)),
+            pl.BlockSpec((512, 512), lambda i: (0, i)),
+            pl.BlockSpec((512, 128), lambda i: (0, 0)),
         ],
         out_specs=pl.BlockSpec((512, 512), lambda i: (0, i)),
         scratch_shapes=[
-            pltpu.VMEM((PW, PW), BF16),
-            pltpu.VMEM((PW, PW), BF16),
-            pltpu.VMEM((512, PW), BF16),
-            pltpu.VMEM((512, PW), BF16),
             pltpu.VMEM((2, 512, 1024), BF16),
             pltpu.VMEM((2, 512, 1024), BF16),
-            pltpu.VMEM((512, 128), F32),
         ],
         name="final",
         compiler_params=params(60),
@@ -733,10 +734,8 @@
         cols,
         received,
         front,
-        own_rows,
-        col_rows,
-        inverse,
-        lower,
+        product,
+        panel,
     )
 
 

time: 139 us -> 139 us (level)
    pallas_call x1, Pallas kernels: 116 us -> 124 us  [body(): pl.pallas_call(panel_kernel, out_shape=(jax.ShapeDtypeStruct((2, NB, 16),...]
    pallas_call x1, Pallas kernels: 21.8 us -> 13.9 us  [body(): pl.pallas_call(final_kernel, out_shape=jax.ShapeDtypeStruct((512, 2048),...]
where the time goes in v6:
time: 139 us
  Pallas kernels  138 us (99%)
    pallas_call x1, Pallas kernels, body(): pl.pallas_call(panel_kernel, out_shape=(jax.ShapeDtypeStruct((2, NB, 16),...  124 us
    pallas_call x1, Pallas kernels, body(): pl.pallas_call(final_kernel, out_shape=jax.ShapeDtypeStruct((512, 2048),...  13.9 us

profile of v6, /device:TPU:132, one launch (start us, length us, event | category | flops | bytes accessed | tf_op | source)
XLA Modules:
  0.0 138.7 jit_solution(13750837379099152975)
XLA Ops:
  0.0 0.6 pad_add_fusion.at_ref
  0.6 124.2 %panel.1 = (s32[2,32,16]{2,1,0:T(8,128)}, s32[2,16,128]{2,1,0:T(8,128)}, f32[512,2048]{1,0:T(8,128)}, f32[512,128]{1,0:T(8,128)}, f32[2,32,24,512]{3,2,1,0:T(8,128)}) custom-call(s32[2,8192]{1,0:T(2,128)} %map_ref.1, f32[512,1024]{1,0:T(8,128)} %bitcast.3, f32[512,2048]{1,0:T(8,128)} %front_ref.3), custom_call_target="tpu_custom_call" | custom-call | flops 30000001024 | bytes 100000000 | tf_op jit(solution)/shard_map/panel/pallas_call | solution.py:656
  124.9 13.9 %final.1 = f32[512,2048]{1,0:T(8,128)} custom-call(s32[2]{0:T(128)} %pad_add_fusion.at_ref, s32[2,32,16]{2,1,0:T(8,128)} %get-tuple-element.10.slot_ref, s32[2,16,128]{2,1,0:T(8,128)} %get-tuple-element.11.col_ref, f32[2,32,24,512]{3,2,1,0:T(8,128)} %get-tuple-element.12.x_ref, f32[512,2048]{1,0:T(8,128)} %front_ref.3, ...), custom_call_target="tpu_custom_call" | custom-call | tf_op jit(solution)/shard_map/final/pallas_call | solution.py:711

commit v7 on v6

--- a/solution.py
+++ b/solution.py
@@ -500,7 +500,11 @@
         rows = exact(inverse, w_ref[pl.ds(at, 128), :], ((1,), (0,)))
         lanes = iota((128, PW), 1)
         ahead = jnp.where(lanes >= at + 128, rows[:, :PW], F32(0.0))
-        w_ref[...] = w_ref[...] - exact(ahead, rows, ((0,), (0,)))
+
+        @pl.when(kb < 3)
+        def _():
+            w_ref[...] = w_ref[...] - exact(ahead, rows, ((0,), (0,)))
+
         w_ref[pl.ds(at, 128), :] = jnp.concatenate([ahead, rows[:, PW:]], axis=1)
         w_ref[pl.ds(at, 128), pl.ds(at, 128)] = upper
 

time: 139 us -> 137 us (0.986)
  Pallas kernels: 138 us -> 136 us
    pallas_call x1, Pallas kernels: 124 us -> 123 us  [body(): pl.pallas_call(panel_kernel, out_shape=(jax.ShapeDtypeStruct((2, NB, 16),...]
where the time goes in v7:
time: 137 us
  Pallas kernels  136 us (99%)
    pallas_call x1, Pallas kernels, body(): pl.pallas_call(panel_kernel, out_shape=(jax.ShapeDtypeStruct((2, NB, 16),...  123 us
    pallas_call x1, Pallas kernels, body(): pl.pallas_call(final_kernel, out_shape=jax.ShapeDtypeStruct((512, 2048),...  13.9 us

profile of v7, /device:TPU:132, one launch (start us, length us, event | category | flops | bytes accessed | tf_op | source)
XLA Modules:
  0.0 137.1 jit_solution(13728886360355577353)
XLA Ops:
  0.0 0.6 pad_add_fusion.at_ref
  0.6 122.6 %panel.1 = (s32[2,32,16]{2,1,0:T(8,128)}, s32[2,16,128]{2,1,0:T(8,128)}, f32[512,2048]{1,0:T(8,128)}, f32[512,128]{1,0:T(8,128)}, f32[2,32,24,512]{3,2,1,0:T(8,128)}) custom-call(s32[2,8192]{1,0:T(2,128)} %map_ref.1, f32[512,1024]{1,0:T(8,128)} %bitcast.3, f32[512,2048]{1,0:T(8,128)} %front_ref.3), custom_call_target="tpu_custom_call" | custom-call | flops 30000001024 | bytes 100000000 | tf_op jit(solution)/shard_map/panel/pallas_call | solution.py:660
  123.3 13.9 %final.1 = f32[512,2048]{1,0:T(8,128)} custom-call(s32[2]{0:T(128)} %pad_add_fusion.at_ref, s32[2,32,16]{2,1,0:T(8,128)} %get-tuple-element.10.slot_ref, s32[2,16,128]{2,1,0:T(8,128)} %get-tuple-element.11.col_ref, f32[2,32,24,512]{3,2,1,0:T(8,128)} %get-tuple-element.12.x_ref, f32[512,2048]{1,0:T(8,128)} %front_ref.3, ...), custom_call_target="tpu_custom_call" | custom-call | tf_op jit(solution)/shard_map/final/pallas_call | solution.py:715

commit v8 on v7

--- a/solution.py
+++ b/solution.py
@@ -244,7 +244,7 @@
     owner = (cmap >> 5) & 7
     slot = owner * 128 + ranks_of(owner, 8, 16)
 
-    def bulk_half(h):
+    def bulk_half(h, high=high, low=low, slot=slot):
         n = iota((512, 1024), 0)
         pick = onehot(slot == (n >> 6) * 128 + h * 64 + (n & 63))
         out = mt(pick, high) + mt(pick, low)
@@ -274,7 +274,6 @@
         each(0, last + 1, one)
 
     bulk_half(0)
-    bulk_half(1)
     owner = (rmap >> 5) & 31
     slot = owner * CAP + ranks_of(owner, 32, 32)
     pick_rows = onehot(slot == iota((32 * CAP, 512), 0))
@@ -301,6 +300,7 @@
 
     each(1, 32, lambda q: to_plane(q).start())
     rows_recv[rg] = rows_send[rg]
+    bulk_half(1)
     total = jnp.where(natural_lower(rg, cg, 512, 128, 0), front_ref[...], F32(0.0))
     picks = [row_picker(slot_ref[child], 16 * CAP) for child in range(2)]
     each(1, 32, lambda q: from_plane(q).wait_recv())

time: 137 us -> 140 us (1.022)
  the two profiles are of different devices: /device:TPU:132 before, /device:TPU:84 now
where the time goes in v8:
time: 140 us
  Pallas kernels  139 us (99%)
    pallas_call x1, Pallas kernels, body(): pl.pallas_call(panel_kernel, out_shape=(jax.ShapeDtypeStruct((2, NB, 16),...  125 us
    pallas_call x1, Pallas kernels, body(): pl.pallas_call(final_kernel, out_shape=jax.ShapeDtypeStruct((512, 2048),...  13.9 us

profile of v8, /device:TPU:84, one launch (start us, length us, event | category | flops | bytes accessed | tf_op | source)
XLA Modules:
  0.0 139.6 jit_solution(10179611155988564989)
XLA Ops:
  0.0 0.6 pad_add_fusion.at_ref
  0.6 125.1 %panel.1 = (s32[2,32,16]{2,1,0:T(8,128)}, s32[2,16,128]{2,1,0:T(8,128)}, f32[512,2048]{1,0:T(8,128)}, f32[512,128]{1,0:T(8,128)}, f32[2,32,24,512]{3,2,1,0:T(8,128)}) custom-call(s32[2,8192]{1,0:T(2,128)} %map_ref.1, f32[512,1024]{1,0:T(8,128)} %bitcast.3, f32[512,2048]{1,0:T(8,128)} %front_ref.3), custom_call_target="tpu_custom_call" | custom-call | flops 30000001024 | bytes 100000000 | tf_op jit(solution)/shard_map/panel/pallas_call | solution.py:660
  125.8 13.9 %final.1 = f32[512,2048]{1,0:T(8,128)} custom-call(s32[2]{0:T(128)} %pad_add_fusion.at_ref, s32[2,32,16]{2,1,0:T(8,128)} %get-tuple-element.10.slot_ref, s32[2,16,128]{2,1,0:T(8,128)} %get-tuple-element.11.col_ref, f32[2,32,24,512]{3,2,1,0:T(8,128)} %get-tuple-element.12.x_ref, f32[512,2048]{1,0:T(8,128)} %front_ref.3, ...), custom_call_target="tpu_custom_call" | custom-call | tf_op jit(solution)/shard_map/final/pallas_call | solution.py:715
